TPU v7x, 128 devices: a whole 4x4x4 slice. The times are simulated.
128 devices in a mesh: seq: 32 (over x, z, core), tp: 4 (over y).
Axes of the slice: x: 4, y: 4, z: 4, core: 2. Of those that a mesh axis runs over, the one named last changes fastest.
Arguments:
- hidden: bfloat16 [4096, 2560], P('seq'), may hold values from -6 to 6
- gain_attn: float32 [2560], replicated, may hold values from 0.5 to 1.5
- w_query: bfloat16 [2560, 2560], P(None, 'tp')
- w_key: bfloat16 [2560, 512], P(None, 'tp'), as said below
- w_value: bfloat16 [2560, 512], P(None, 'tp'), may hold values from -0.125 to 0.125
- w_out: bfloat16 [2560, 2560], P('tp'), may hold values from -0.125 to 0.125
- gain_moe: float32 [2560], replicated, may hold values from 0.5 to 1.5
- expert_ids: int32 [4096, 6], P('seq'), may hold values from 0 to 63, all different within a row; in each aligned block of 128 rows (0 to 127, 128 to 255, ...) at most 24 rows name the same one
- expert_gates: float32 [4096, 6], P('seq'), may hold values from 0.05 to 0.3
- w_gate: bfloat16 [64, 2560, 1536], P('seq', None, 'tp'), may hold values from -0.125 to 0.125
- w_up: bfloat16 [64, 2560, 1536], P('seq', None, 'tp'), may hold values from -0.125 to 0.125
- w_down: bfloat16 [64, 1536, 2560], P('seq', 'tp'), may hold values from -0.15625 to 0.15625
- seg_lengths: int32 [16], replicated, may hold values from 1 to 1024, 4096 in all
- slot_page: int32 [2048], replicated, may hold values from -1 to 255, as said below
Outputs:
- hidden_out: bfloat16 [4096, 2560], P('seq', 'tp')
- kv_cache: bfloat16 [2048, 16, 1024], P('seq', None, 'tp')
Inputs may be any that keep to these rules, and one draw needn't show every extreme that they name: `expert_ids`: a row names 6 different experts; within the 128 rows of one index of seq no expert is named by more than 24 rows. `seg_lengths`: segment lengths in order, summing to 4096. `slot_page`: owner o holds slots o * 64 to o * 64 + 63 as 2 requests of 32 slots; a request lists 1 to 32 consecutive pages (after the last page comes page 0), then -1 in its remaining slots. `w_key`: key projection of fan-in scale.
All inputs are finite; a program needn't handle non-finite values.
Results may differ from a plain program's by a relative error of at most 0.015.
Values may be sent and summed in bfloat16 or wider, within the bound.
A program may use at most 192 MiB of HBM per device.

v0:
```python
import math

import jax
import jax.numpy as jnp
from jax import lax
from jax.sharding import PartitionSpec as P

HEAD_DIM = 128
TOP = 6
PAGE = 16


epsilon = 1e-05
rope_base = 500000.0
masked_score = -1e30


def rms_norm(values, gain_vec):
    widened = values.astype(jnp.float32)
    factor = lax.rsqrt(jnp.mean(widened * widened, axis=-1, keepdims=True) + epsilon)
    return (widened * factor * gain_vec).astype(jnp.bfloat16)


def rotate(values, position):
    half_dim = values.shape[-1] // 2
    inverse = rope_base ** (-2.0 * jnp.arange(half_dim, dtype=jnp.float32) / values.shape[-1])
    angles = position.astype(jnp.float32)[:, None] * inverse[None, :]
    cosine = jnp.cos(angles)[:, None, :]
    sine_part = jnp.sin(angles)[:, None, :]
    first_half = values[..., :half_dim]
    second_half = values[..., half_dim:]
    return jnp.concatenate(
        [
            first_half * cosine - second_half * sine_part,
            second_half * cosine + first_half * sine_part,
        ],
        axis=-1,
    )


def segment_start(seg_lengths, positions):
    bounds = jnp.cumsum(seg_lengths)
    starts = bounds - seg_lengths
    return jnp.max(jnp.where(starts[None, :] <= positions[:, None], starts[None, :], 0), axis=1)


def over_blocks(step_fn, carried, portion, key_positions):
    rows = portion.shape[0]
    size = math.gcd(rows, 512)
    count = rows // size
    stacked = portion.reshape((count, size) + portion.shape[1:])
    pos_stack = key_positions.reshape(count, size)

    def turn(state, item):
        return (step_fn(state, item[0], item[1]), None)

    carried, unused = lax.scan(turn, carried, (stacked, pos_stack))
    return carried


def attend_piece(
    soft_state,
    queries,
    piece_keys,
    piece_values,
    key_positions,
    query_positions,
    query_first,
    scaling,
):
    running_max, row_total, accum_sum = soft_state
    scores = (
        jnp.einsum("qkgd,skd->qkgs", queries, piece_keys, preferred_element_type=jnp.float32)
        * scaling
    )
    allowed = (key_positions[None, :] <= query_positions[:, None]) & (
        key_positions[None, :] >= query_first[:, None]
    )
    allowed = allowed[:, None, None, :]
    scores = jnp.where(allowed, scores, masked_score)
    new_max = jnp.maximum(running_max, jnp.max(scores, axis=-1))
    weights = jnp.where(allowed, jnp.exp(scores - new_max[..., None]), 0.0)
    rescale = jnp.exp(running_max - new_max)
    row_total = row_total * rescale + jnp.sum(weights, axis=-1)
    product = jnp.einsum(
        "qkgs,skd->qkgd",
        weights.astype(jnp.bfloat16),
        piece_values,
        preferred_element_type=jnp.float32,
    )
    accum_sum = accum_sum * rescale[..., None] + product
    return (new_max, row_total, accum_sum)


def local(
    hidden,
    gain_attn,
    w_query,
    w_key,
    w_value,
    w_out,
    gain_moe,
    expert_ids,
    expert_gates,
    w_gate,
    w_up,
    w_down,
    seg_lengths,
    slot_page,
):
    tok_rows = hidden.shape[0]
    model_width = hidden.shape[1]
    shard_count = lax.axis_size("seq")
    shard_index = lax.axis_index("seq")
    tensor_index = lax.axis_index("tp")
    quarter = model_width // lax.axis_size("tp")
    kv_local = w_key.shape[1] // HEAD_DIM
    q_local = w_query.shape[1] // HEAD_DIM
    group_size = q_local // kv_local
    positions = shard_index * tok_rows + jnp.arange(tok_rows, dtype=jnp.int32)
    seg_first = segment_start(seg_lengths, positions)
    offsets = positions - seg_first
    normed = rms_norm(hidden, gain_attn)
    query_raw = jnp.dot(normed, w_query, preferred_element_type=jnp.float32).reshape(
        tok_rows, q_local, HEAD_DIM
    )
    queries = (
        rotate(query_raw, offsets)
        .astype(jnp.bfloat16)
        .reshape(tok_rows, kv_local, group_size, HEAD_DIM)
    )
    key_raw = jnp.dot(normed, w_key, preferred_element_type=jnp.float32).reshape(
        tok_rows, kv_local, HEAD_DIM
    )
    keys_rot = rotate(key_raw, offsets).astype(jnp.bfloat16)
    values = (
        jnp.dot(normed, w_value, preferred_element_type=jnp.float32)
        .astype(jnp.bfloat16)
        .reshape(tok_rows, kv_local, HEAD_DIM)
    )
    kv_rows = jnp.stack([keys_rot, values], axis=2)
    row_width = 2 * kv_local * HEAD_DIM
    slot_count = slot_page.shape[0] // shard_count
    own_slots = lax.dynamic_slice_in_dim(slot_page, shard_index * slot_count, slot_count)
    wanted = own_slots[:, None, None] * PAGE + jnp.arange(PAGE, dtype=jnp.int32)[None, :, None]
    scaling = HEAD_DIM ** (-0.5)
    empty_max = jnp.full((tok_rows, kv_local, group_size), masked_score, jnp.float32)
    empty_total = jnp.zeros((tok_rows, kv_local, group_size), jnp.float32)
    empty_sum = jnp.zeros((tok_rows, kv_local, group_size, HEAD_DIM), jnp.float32)
    empty_cache = jnp.zeros((slot_count, PAGE, row_width), jnp.float32)

    def cache_rows(cache_acc, portion, key_positions):
        piece_rows = portion.shape[0]
        chosen = (wanted == key_positions[None, None, :]).astype(jnp.bfloat16)
        return cache_acc + jnp.einsum(
            "spc,cw->spw",
            chosen,
            portion.reshape(piece_rows, row_width),
            preferred_element_type=jnp.float32,
        )

    def attend_rows(soft_state, portion, key_positions):
        return attend_piece(
            soft_state,
            queries,
            portion[:, :, 0],
            portion[:, :, 1],
            key_positions,
            positions,
            seg_first,
            scaling,
        )

    def both_rows(carried, portion, key_positions):
        soft_state, cache_acc = carried
        return (
            attend_rows(soft_state, portion, key_positions),
            cache_rows(cache_acc, portion, key_positions),
        )

    portion = lax.all_gather(kv_rows, "seq", axis=0, tiled=True)
    key_positions = jnp.arange(portion.shape[0], dtype=jnp.int32)
    soft_state, cache_acc = over_blocks(
        both_rows, ((empty_max, empty_total, empty_sum), empty_cache), portion, key_positions
    )
    running_max, row_total, accum_sum = soft_state
    attended = (
        (accum_sum / row_total[..., None])
        .astype(jnp.bfloat16)
        .reshape(tok_rows, q_local * HEAD_DIM)
    )
    kv_cache = cache_acc.astype(jnp.bfloat16)
    partial_value = jnp.dot(attended, w_out, preferred_element_type=jnp.float32)
    exp_local = w_gate.shape[0]
    experts_all = exp_local * shard_count
    capacity = (tok_rows * TOP * 3 // (2 * experts_all) + 7) // 8 * 8
    flat_ids = expert_ids.reshape(tok_rows * TOP)
    expert_hits = (flat_ids[:, None] == jnp.arange(experts_all, dtype=jnp.int32)[None, :]).astype(
        jnp.int32
    )
    slot_rank = jnp.sum((jnp.cumsum(expert_hits, axis=0) - 1) * expert_hits, axis=1)
    target = flat_ids * capacity + slot_rank
    places = (
        jnp.arange(experts_all * capacity, dtype=jnp.int32)[:, None, None]
        == target.reshape(tok_rows, TOP)[None, :, :]
    )
    selector = jnp.any(places, axis=2).astype(jnp.bfloat16)
    attn_full = lax.psum(partial_value.astype(jnp.bfloat16), "tp").astype(jnp.float32)
    mid = (hidden.astype(jnp.float32) + attn_full).astype(jnp.bfloat16)
    moe_in = rms_norm(mid, gain_moe)
    residual = lax.dynamic_slice_in_dim(mid, tensor_index * quarter, quarter, 1)
    packed = jnp.dot(selector, moe_in, preferred_element_type=jnp.float32).astype(jnp.bfloat16)
    rows_in = lax.all_to_all(
        packed.reshape(shard_count, exp_local, capacity, moe_in.shape[1]),
        "seq",
        split_axis=0,
        concat_axis=0,
        tiled=True,
    )
    gate_term = jnp.einsum("secd,edf->secf", rows_in, w_gate, preferred_element_type=jnp.float32)
    up_term = jnp.einsum("secd,edf->secf", rows_in, w_up, preferred_element_type=jnp.float32)
    hidden_act = (jax.nn.silu(gate_term) * up_term).astype(jnp.bfloat16)
    down_term = jnp.einsum("secf,efd->secd", hidden_act, w_down, preferred_element_type=jnp.float32)
    merged = lax.psum_scatter(down_term.astype(jnp.bfloat16), "tp", scatter_dimension=3, tiled=True)
    returned = lax.all_to_all(merged, "seq", split_axis=0, concat_axis=0, tiled=True)
    flat_back = returned.reshape(experts_all * capacity, quarter)
    picked = jnp.take(flat_back, target, axis=0).astype(jnp.float32).reshape(tok_rows, TOP, quarter)
    moe_out = jnp.einsum("tk,tkd->td", expert_gates, picked)
    final_rows = (residual.astype(jnp.float32) + moe_out).astype(jnp.bfloat16)
    return (final_rows, kv_cache)


def solution(mesh):
    placed = (
        P("seq", None),
        P(),
        P(None, "tp"),
        P(None, "tp"),
        P(None, "tp"),
        P("tp", None),
        P(),
        P("seq", None),
        P("seq", None),
        P("seq", None, "tp"),
        P("seq", None, "tp"),
        P("seq", "tp", None),
        P(),
        P(),
    )
    return jax.shard_map(
        local,
        mesh=mesh,
        in_specs=placed,
        out_specs=(P("seq", "tp"), P("seq", None, "tp")),
        check_vma=False,
    )
```

profile of v0, /device:TPU:0, one launch (start us, length us, event | category | flops | bytes accessed | tf_op | source)
XLA Modules:
  0.0 592.4 jit_solution(5520721394446283536)
XLA Ops:
  17.0 3.6 fusion.80
  23.4 40.0 %all-gather.2.cloned.1.call-done = bf16[4096,1,2,128]{0,3,2,1:T(8,128)(2,1)} async-done(((bf16[128,1,2,128]{0,3,2,1:T(8,128)(2,1)}), bf16[4096,1,2,128]{0,3,2,1:T(8,128)(2,1)}) %all-gather.2.cloned.1.call-update) | async-done | bytes 2097168 | tf_op jit(solution)/shard_map/all_gather | solution.py:181
  63.4 3.8 copy.103
  67.1 4.5 copy.78
  71.7 104.9 %while.17 = (s32[]{:T(128)}, f32[128,1,5]{0,2,1:T(8,128)S(1)}, f32[128,1,5]{0,2,1:T(8,128)S(1)}, f32[128,1,5,128]{0,3,2,1:T(8,128)}, f32[64,16,256]{2,1,0:T(8,12...) while((s32[]{:T(128)}, f32[128,1,5]{0,2,1:T(8,128)S(1)}, ...), condition=%wide.region_6.7_spmd.clone, body=%wide.region_3.6_spmd.clone.sunk | while | flops 440652672 | bytes 13333522 | solution.py:57
  92.7 2.9 fusion.113
  105.8 2.9 fusion.113
  132.1 2.9 fusion.113
  145.3 2.9 fusion.113
  171.6 2.9 fusion.113
  182.8 39.6 %all-reduce.2.cloned.1.call-done = bf16[128,2560]{1,0:T(8,128)(2,1)} async-done(((bf16[128,2560]{1,0:T(8,128)(2,1)}), bf16[128,2560]{1,0:T(8,128)(2,1)}) %all-reduce.2.cloned.1.call-update) | async-done | bytes 655376 | tf_op jit(solution)/shard_map/psum | solution.py:208
  226.1 97.1 %all_to_all.10 = bf16[32,2,24,2560]{3,2,1,0:T(8,128)(2,1)S(1)} all-to-all(bf16[32,2,24,2560]{3,2,1,0:T(8,128)(2,1)S(1)} %bitcast.173), channel_id=1, replica_groups=mesh['seq'=32,'tp'=4] {'seq'}, dimensions={0} | all-to-all | bytes 15728640 | tf_op jit(solution)/shard_map/all_to_all | solution.py:213
  323.2 3.1 copy-done.6
  326.3 4.4 fusion.26
  330.7 13.8 %convert_bitcast_fusion = bf16[32,2,24,2560]{3,2,0,1:T(8,128)(2,1)} fusion(bf16[2,384,2560]{2,1,0:T(8,128)(2,1)} %param.27, f32[2,32,24,384]{3,2,1,0:T(8,128)S(1)} %fusion.26, bf16[2,2560,384]{2,1,0:T(8,128)(2,1)} %param.26, bf16[32,2,24,2560]{3,2,1,0:T(8,128)(2,1)} %copy-done.6), kind=kOutput, calls=%fused_computation.36 | convolution fusion | flops 6047268864 | bytes 25952256 | tf_op jit(solution)/shard_map/secf,efd->secd/dot_general | solution.py:223
  344.6 35.5 %copy.99 = bf16[32,2,24,2560]{2,0,1,3:T(8,128)(2,1)} copy(bf16[32,2,24,2560]{3,2,0,1:T(8,128)(2,1)} %convert_bitcast_fusion) | data formatting | bytes 15728640
  380.1 57.5 %reshape.481 = bf16[2560,1536]{1,0:T(8,128)(2,1)} reshape(bf16[2560,2,32,24]{3,2,1,0:T(8,128)(2,1)} %bitcast.172) | data formatting | bytes 15728640
  437.6 74.6 %reduce-scatter.4.cloned.1.call-done = bf16[640,1536]{1,0:T(8,128)(2,1)} async-done(((bf16[2560,1536]{1,0:T(8,128)(2,1)}), bf16[640,1536]{1,0:T(8,128)(2,1)}) %reduce-scatter.4.cloned.1.call-update) | async-done | bytes 1966096
  512.2 18.8 %reshape.482 = bf16[640,2,32,24]{3,2,1,0:T(8,128)(2,1)} reshape(bf16[640,1536]{1,0:T(8,128)(2,1)} %reduce-scatter.4.cloned.1.call-done) | data formatting | bytes 3932160
  531.0 10.0 %copy.87 = bf16[32,2,24,640]{3,2,1,0:T(8,128)(2,1)} copy(bf16[32,2,24,640]{2,0,1,3:T(8,128)(2,1)} %bitcast.175) | data formatting | bytes 3932160 | tf_op jit(solution)/shard_map/reduce_scatter | solution.py:224
  541.1 7.4 %all-to-all-start.1 = ((bf16[32,2,24,640]{3,2,1,0:T(8,128)(2,1)}), bf16[32,2,24,640]{3,2,1,0:T(8,128)(2,1)S(1)}, u32[]{:S(2)}, u32[]{:S(2)}) async-start(bf16[32,2,24,640]{3,2,1,0:T(8,128)(2,1)} %copy.87), calls=%async_computation.1 | async-start | bytes 3932160 | tf_op jit(solution)/shard_map/all_to_all | solution.py:225
  550.0 26.0 %all-to-all-done.1 = bf16[32,2,24,640]{3,2,1,0:T(8,128)(2,1)S(1)} async-done(((bf16[32,2,24,640]{3,2,1,0:T(8,128)(2,1)}), bf16[32,2,24,640]{3,2,1,0:T(8,128)(2,1)S(1)}, u32[]{:S(2)}, u32[]{:S(2)}) %all-to-all-start.1) | async-done | bytes 1966112 | tf_op jit(solution)/shard_map/all_to_all | solution.py:225
  575.9 3.4 gather_fusion
  579.4 2.9 gather.7
  (263 shorter events, 117.2 us)
Async XLA Ops:
  7.2 170.5 %copy-start = (bf16[640,2560]{1,0:T(8,128)(2,1)S(1)}, bf16[640,2560]{1,0:T(8,128)(2,1)}, u32[]{:S(2)}) copy-start(bf16[640,2560]{1,0:T(8,128)(2,1)} %param.21) | copy-start | bytes 9830404
  7.2 6.1 %copy-start.14 = (f32[2560]{0:T(1024)S(1)}, f32[2560]{0:T(1024)}, u32[]{:S(2)}) copy-start(f32[2560]{0:T(1024)} %param.17) | copy-start | bytes 30724
  7.2 8.8 %copy-start.12 = (s32[128,6]{0,1:T(8,128)S(1)}, s32[128,6]{0,1:T(8,128)}, u32[]{:S(2)}) copy-start(s32[128,6]{0,1:T(8,128)} %param.23) | copy-start | bytes 9220
  7.2 56.2 %all-gather.2.cloned.1.call-start = ((), (), s32[]{:S(2)}) async-start(), calls=%async_computation.3 | async-start | bytes 2162688 | tf_op jit(solution)/shard_map/all_gather | solution.py:181
  15.9 206.5 %all-reduce.2.cloned.1.call-start = ((), (), s32[]{:S(2)}) async-start(), calls=%async_computation.4 | async-start | bytes 1310720 | tf_op jit(solution)/shard_map/psum | solution.py:208
  16.1 4.5 copy-start.10
  92.6 2.9 copy-start.3
  92.7 2.9 copy-start.7
  105.8 2.9 copy-start.3
  105.8 2.9 copy-start.7
  132.1 2.9 copy-start.3
  132.1 2.9 copy-start.7
  145.3 2.9 copy-start.3
  145.3 2.9 copy-start.7
  171.6 2.9 copy-start.7
  179.2 43.2 %copy-start.8 = (bf16[128,2560]{1,0:T(8,128)(2,1)S(1)}, bf16[128,2560]{1,0:T(8,128)(2,1)}, u32[]{:S(2)}) copy-start(bf16[128,2560]{1,0:T(8,128)(2,1)} %param.16) | copy-start | bytes 1966084
  179.2 44.6 %copy-start.15 = (f32[2560]{0:T(1024)S(1)}, f32[2560]{0:T(1024)}, u32[]{:S(2)}) copy-start(f32[2560]{0:T(1024)} %param.22) | copy-start | bytes 30724
  179.2 333.0 %reduce-scatter.4.cloned.1.call-start = ((), (), s32[]{:S(2)}) async-start(), calls=%async_computation.5 | async-start | bytes 9830400
  226.1 100.2 %copy-start.17 = (bf16[2,2560,384]{2,1,0:T(8,128)(2,1)S(1)}, bf16[2,2560,384]{2,1,0:T(8,128)(2,1)}, u32[]{:S(2)}) copy-start(bf16[2,2560,384]{2,1,0:T(8,128)(2,1)} %param.25) | copy-start | bytes 11796484
  323.2 3.1 copy-start.6
  541.1 7.7 %copy-start.16 = (f32[128,6]{0,1:T(8,128)S(1)}, f32[128,6]{0,1:T(8,128)}, u32[]{:S(2)}) copy-start(f32[128,6]{0,1:T(8,128)} %param.24) | copy-start | bytes 9220
  541.1 8.0 %copy-start.2 = (f32[64,16,256]{2,1,0:T(8,128)S(1)}, f32[64,16,256]{2,1,0:T(8,128)}, u32[]{:S(2)}) copy-start(f32[64,16,256]{2,1,0:T(8,128)} %get-tuple-element.63) | copy-start | bytes 3145732
  541.1 34.9 %all-to-all-start.1 = ((bf16[32,2,24,640]{3,2,1,0:T(8,128)(2,1)}), bf16[32,2,24,640]{3,2,1,0:T(8,128)(2,1)S(1)}, u32[]{:S(2)}, u32[]{:S(2)}) async-start(bf16[32,2,24,640]{3,2,1,0:T(8,128)(2,1)} %copy.87), calls=%async_computation.1 | async-start | bytes 3932160 | tf_op jit(solution)/shard_map/all_to_all | solution.py:225
  579.4 6.5 %copy-start.1 = (bf16[640,2560]{1,0:T(8,128)(2,1)S(1)}, bf16[640,2560]{1,0:T(8,128)(2,1)}, u32[]{:S(2)}) copy-start(bf16[640,2560]{1,0:T(8,128)(2,1)} %param.21) | copy-start | bytes 9830404
  (26 other events, 38.9 us)
Sparse Core Ops, SparseCore 0:
  16.0 47.3 all-gather.1
  179.4 42.9 all-reduce.1
  437.8 74.4 reduce-scatter.3
where the time goes:
time: 598 us; the launch traced here: 592 us
  local copies, waits for them, and re-layouts  195 us (33%)
  waiting for transfers between devices  180 us (30%)
  blocking collectives  97.1 us (16%)
  matrix products  59.8 us (10%)
  other arithmetic  37.6 us (6%)
  between operations  14.1 us (2%)
  starting transfers between devices  7.5 us (1%)
    unnamed x36, local copies, waits for them, and re-layouts  124 us
    all_to_all x1, blocking collectives, local(): lax.all_to_all(packed.reshape(shard_count, exp_local, capacity, moe_in.sh...  97.1 us
    unnamed x4, waiting for transfers between devices  74.6 us
    all_gather x1, waiting for transfers between devices, local(): portion = lax.all_gather(kv_rows, 'seq', axis=0, tiled=True)  40 us
    psum x1, waiting for transfers between devices, local(): lax.psum(partial_value.astype(jnp.bfloat16), 'tp').astype(jnp.float32)  39.6 us
    all_to_all x1, waiting for transfers between devices, local(): lax.all_to_all(merged, 'seq', split_axis=0, concat_axis=0, tiled=True)  26 us
    dot_general x8, matrix products, cache_rows(): jnp.einsum('spc,cw->spw', chosen, portion.reshape(piece_rows, row_width),...  22.8 us
    dynamic_slice x24, local copies, waits for them, and re-layouts, over_blocks(): carried, unused = lax.scan(turn, carried, (stacked, pos_stack))  21.4 us
  transfers between devices with their start and end apart: 4, of which 4 were waited for; matrix products, arithmetic and copies ran while one was open for 2% of the time, Pallas kernels for 0%

commit v1 on v0

v1 whole, which is shorter than its diff:
```python
import functools

import jax
import jax.numpy as jnp
from jax import lax
from jax.experimental import pallas as pl
from jax.experimental.pallas import tpu as pltpu
from jax.sharding import PartitionSpec as P

HEAD_DIM = 128
TOP = 6
PAGE = 16
CAP = 24
RING = 4
MESH = pl.DeviceIdType.MESH
ANY = pl.BlockSpec(memory_space=pl.ANY)
WHOLE = pl.BlockSpec(memory_space=pltpu.VMEM)
epsilon = 1e-05
rope_base = 500000.0
masked_score = -1e30
bf16 = jnp.bfloat16
f32 = jnp.float32


def my_place():
    index = lax.axis_index("seq")
    return {
        "x": index // 8,
        "z": lax.rem(index // 2, RING),
        "c": lax.rem(index, 2),
        "y": lax.axis_index("tp"),
    }


def device_at(place):
    return ((place["x"] * RING + place["z"]) * 2 + place["c"], place["y"])


def moved(place, axis, step):
    size = 2 if axis == "c" else RING
    other = dict(place)
    other[axis] = lax.rem(place[axis] + step + size, size)
    return other


def enter(places):
    barrier = pltpu.get_barrier_semaphore()
    for place in places:
        pl.semaphore_signal(barrier, inc=1, device_id=device_at(place), device_id_type=MESH)
    pl.semaphore_wait(barrier, len(places))


class Links:
    def __init__(self, send_sem, recv_sem):
        self.send_sem, self.recv_sem, self.count = send_sem, recv_sem, 0
        self.started = []

    def push(self, src, dst, place):
        copy = pltpu.make_async_remote_copy(
            src_ref=src,
            dst_ref=dst,
            send_sem=self.send_sem.at[self.count],
            recv_sem=self.recv_sem.at[self.count],
            device_id=device_at(place),
            device_id_type=MESH,
        )
        self.count += 1
        copy.start()
        self.started.append(copy)
        return copy

    def finish(self):
        for copy in self.started:
            copy.wait_send()


def torus_gather(me, dims, parts, src, out, links, local_sem):
    sibling = moved(me, "c", 1)

    def at(where, row0, rows):
        return out.at[tuple(where[d] for d in dims) + (pl.ds(row0, rows), slice(None))]

    own = {d: me[d] for d in dims}
    local = pltpu.make_async_copy(src, at(own, 0, src.shape[0]), local_sem)
    local.start()
    to_sibling = [links.push(src, at(own, 0, src.shape[0]), sibling)]
    for phase in range(len(parts[0][3])):
        if phase == 1:
            local.wait()
        live = []
        for row0, rows, half, order in parts:
            axis = order[phase]
            base = dict(own)
            for done in order[:phase]:
                base[done] = slice(None)
            whole = at(base, row0, rows)
            source = src.at[pl.ds(row0, rows), :] if phase == 0 else whole
            up = links.push(source, whole, moved(me, axis, 1))
            down = links.push(source, whole, moved(me, axis, -1))
            live.append((row0, rows, half, order, axis, base, up, down))
        forwarded = []
        for row0, rows, half, order, axis, base, up, down in live:
            for copy, step in ((up, 1), (down, -1)):
                copy.wait_recv()
                got = dict(base)
                got[axis] = moved(me, axis, -step)[axis]
                if phase == 0:
                    r0, rn = (row0, half) if step == 1 else (row0 + half, rows - half)
                    piece = at(got, r0, rn)
                else:
                    cut = dict(got)
                    cut[order[0]] = pl.ds(0, 2) if step == 1 else pl.ds(2, 2)
                    piece = at(cut, row0, rows)
                forwarded.append(links.push(piece, piece, moved(me, axis, step)))
                there = at(got, row0, rows)
                to_sibling.append(links.push(there, there, sibling))
        for n, (row0, rows, half, order, axis, base, up, down) in enumerate(live):
            forwarded[2 * n].wait_recv()
            forwarded[2 * n + 1].wait_recv()
            got = dict(base)
            got[axis] = moved(me, axis, 2)[axis]
            there = at(got, row0, rows)
            to_sibling.append(links.push(there, there, sibling))
    for copy in to_sibling:
        copy.wait_recv()


def copies_of_gather(parts):
    phases = len(parts[0][3])
    return 1 + phases * len(parts) * 7


KV_PARTS = ((0, 80, 48, ("x", "z")), (80, 64, 32, ("z", "x")))
ROW_PARTS = (
    (0, 48, 32, ("z", "y", "x")),
    (48, 48, 32, ("y", "x", "z")),
    (96, 32, 16, ("x", "z", "y")),
)


def kv_gather_kernel(src, out, send_sem, recv_sem, local_sem):
    me = my_place()
    enter([moved(me, a, s) for a in ("x", "z") for s in (1, -1)] + [moved(me, "c", 1)])
    links = Links(send_sem, recv_sem)
    torus_gather(me, ("x", "z", "c"), KV_PARTS, src, out, links, local_sem)
    links.finish()


def kv_gather(rows):
    n = copies_of_gather(KV_PARTS)
    return pl.pallas_call(
        kv_gather_kernel,
        out_shape=jax.ShapeDtypeStruct((RING, RING, 2) + rows.shape, bf16),
        in_specs=[ANY],
        out_specs=ANY,
        scratch_shapes=[
            pltpu.SemaphoreType.DMA((n,)),
            pltpu.SemaphoreType.DMA((n,)),
            pltpu.SemaphoreType.DMA,
        ],
        compiler_params=pltpu.CompilerParams(collective_id=1, has_side_effects=True),
        name="kv_gather",
    )(rows)


def row_gather_kernel(
    terms, hidden, gain, out, mid, heard, squares, mid_v, row_v, send_sem, recv_sem, local_sem
):
    me = my_place()
    peers = [moved(me, "y", s) for s in (1, 2, 3)]
    enter(
        [moved(me, a, s) for a in ("x", "z") for s in (1, -1)] + [moved(me, "c", 1)] + peers
    )
    links = Links(send_sem, recv_sem)
    sent = [
        links.push(terms.at[peer["y"]], heard.at[n], peer) for n, peer in enumerate(peers)
    ]
    total = terms[me["y"]].astype(f32)
    for n in range(3):
        sent[n].wait_recv()
        total = total + heard[n].astype(f32)
    mid_now = (hidden[...].astype(f32) + total).astype(bf16)
    mid_v[...] = mid_now
    wide = mid_now.astype(f32)
    ours = jnp.sum(wide * wide, axis=1, keepdims=True)
    squares[3] = jnp.broadcast_to(ours, (ours.shape[0], 128))
    told = [links.push(squares.at[3], squares.at[n], peer) for n, peer in enumerate(peers)]
    whole = ours
    for n in range(3):
        told[n].wait_recv()
        whole = whole + squares[n][:, :1]
    factor = lax.rsqrt(whole * (1.0 / (RING * wide.shape[1])) + epsilon)
    row_v[...] = (wide * factor * gain[...]).astype(bf16)
    keep = pltpu.make_async_copy(mid_v, mid, local_sem.at[1])
    keep.start()
    torus_gather(me, ("x", "z", "c", "y"), ROW_PARTS, row_v, out, links, local_sem.at[0])
    keep.wait()
    links.finish()


def row_gather(terms, hidden, gain):
    n = 6 + copies_of_gather(ROW_PARTS)
    rows, cols = hidden.shape
    return pl.pallas_call(
        row_gather_kernel,
        out_shape=(
            jax.ShapeDtypeStruct((RING, RING, 2, RING, rows, cols), bf16),
            jax.ShapeDtypeStruct((rows, cols), bf16),
        ),
        in_specs=[WHOLE, WHOLE, WHOLE],
        out_specs=(ANY, ANY),
        scratch_shapes=[
            pltpu.VMEM((3, rows, cols), bf16),
            pltpu.VMEM((4, rows, 128), f32),
            pltpu.VMEM((rows, cols), bf16),
            pltpu.VMEM((rows, cols), bf16),
            pltpu.SemaphoreType.DMA((n,)),
            pltpu.SemaphoreType.DMA((n,)),
            pltpu.SemaphoreType.DMA((2,)),
        ],
        compiler_params=pltpu.CompilerParams(
            collective_id=2, has_side_effects=True, vmem_limit_bytes=16 << 20
        ),
        name="row_gather",
    )(terms, hidden, gain)


SUM_ORDERS = (("x", "y", "z"), ("z", "x", "y"), ("y", "z", "x"))
SUM_DIMS = ("x", "z", "y")


def row_sum_kernel(terms, mid, out, total, other, bufs, out_v, send_sem, recv_sem, local_sem):
    me = my_place()
    sibling = moved(me, "c", 1)
    enter([moved(me, a, s) for a in ("x", "z", "y") for s in (1, -1)] + [sibling])
    links = Links(send_sem, recv_sem)
    spans = [(row0, rows, half) for row0, rows, half, _ in ROW_PARTS]
    cols = out.shape[1]

    def held(ref, where, row0, rows):
        return ref.at[tuple(where[d] for d in SUM_DIMS) + (pl.ds(row0, rows), slice(None))]

    def add(where, row0, rows, buf):
        open_dims = [d for d in SUM_DIMS if isinstance(where[d], tuple)]
        sizes = [where[d][1] for d in open_dims]
        count = 1
        for size in sizes:
            count *= size

        def one(step, carry):
            rest, picks = step, []
            for size in reversed(sizes):
                picks.append(lax.rem(rest, size))
                rest = rest // size
            picks = picks[::-1]
            place = dict(where)
            for d, pick in zip(open_dims, picks):
                place[d] = where[d][0] + pick
            index = tuple(place[d] for d in SUM_DIMS) + (pl.ds(row0, rows), slice(None))
            total[index] = (total[index].astype(f32) + buf[tuple(picks)].astype(f32)).astype(bf16)
            return carry

        lax.fori_loop(0, count, one, 0)

    full = (0, RING)

    def sliced(where):
        return {d: pl.ds(*v) if isinstance(v, tuple) else v for d, v in where.items()}

    first = []
    slots = 0
    for step in (2, 1, 3, 0):
        for (row0, rows, half), order in zip(spans, SUM_ORDERS):
            where = {d: full for d in SUM_DIMS}
            where[order[0]] = moved(me, order[0], step)[order[0]]
            cut = sliced(where)
            mine = (cut["x"], cut["z"], me["c"], cut["y"], pl.ds(row0, rows), slice(None))
            theirs = (cut["x"], cut["z"], sibling["c"], cut["y"], pl.ds(row0, rows), slice(None))
            keep = pltpu.make_async_copy(
                terms.at[mine], held(total, cut, row0, rows), local_sem.at[slots]
            )
            keep.start()
            slots += 1
            push = links.push(terms.at[theirs], held(other, cut, row0, rows), sibling)
            first.append((where, row0, rows, keep, push))

    def settle(step, part):
        where, row0, rows, keep, push = first[(2, 1, 3, 0).index(step) * 3 + part]
        keep.wait()
        push.wait_recv()
        open_dims = [d for d in SUM_DIMS if isinstance(where[d], tuple)]

        def one(n, carry):
            place = dict(where)
            place[open_dims[0]] = n // RING
            place[open_dims[1]] = lax.rem(n, RING)
            index = tuple(place[d] for d in SUM_DIMS) + (pl.ds(row0, rows), slice(None))
            total[index] = (total[index].astype(f32) + other[index].astype(f32)).astype(bf16)
            return carry

        lax.fori_loop(0, RING * RING, one, 0)

    for phase in range(3):
        live = []
        for part, ((row0, rows, half), order) in enumerate(zip(spans, SUM_ORDERS)):
            axis = order[phase]
            base = {d: me[d] for d in SUM_DIMS}
            for later in order[phase + 1 :]:
                base[later] = full
            far, up, down = (moved(me, axis, s)[axis] for s in (2, 1, -1))
            buf_a, buf_b, buf_p, buf_m = bufs[(phase * 3 + part) * 4 : (phase * 3 + part) * 4 + 4]
            if phase == 0:
                settle(2, part)

            def half_of(index, which, base=base, axis=axis, order=order, row0=row0, rows=rows, half=half, phase=phase):
                where = dict(base)
                where[axis] = index
                if phase == 2:
                    r0, rn = (row0, half) if which == 0 else (row0 + half, rows - half)
                    return where, r0, rn
                where[order[phase + 1]] = (0, 2) if which == 0 else (2, 2)
                return where, row0, rows

            whole_of = lambda index, base=base, axis=axis: {**base, axis: index}
            where, r0, rn = half_of(far, 0)
            send_a = links.push(held(total, sliced(where), r0, rn), buf_a, moved(me, axis, 1))
            where, r0, rn = half_of(far, 1)
            send_b = links.push(held(total, sliced(where), r0, rn), buf_b, moved(me, axis, -1))
            live.append((row0, rows, axis, up, down, half_of, whole_of, send_a, send_b, buf_a, buf_b, buf_p, buf_m))
        second = []
        for part, (row0, rows, axis, up, down, half_of, whole_of, send_a, send_b, buf_a, buf_b, buf_p, buf_m) in enumerate(live):
            if phase == 0:
                settle(1, part)
            send_a.wait_recv()
            add(*half_of(up, 0), buf_a)
            push_p = links.push(held(total, sliced(whole_of(up)), row0, rows), buf_p, moved(me, axis, 1))
            if phase == 0:
                settle(3, part)
            send_b.wait_recv()
            add(*half_of(down, 1), buf_b)
            push_m = links.push(held(total, sliced(whole_of(down)), row0, rows), buf_m, moved(me, axis, -1))
            second.append((push_p, push_m))
        for part, (row0, rows, axis, up, down, half_of, whole_of, send_a, send_b, buf_a, buf_b, buf_p, buf_m) in enumerate(live):
            if phase == 0:
                settle(0, part)
            push_p, push_m = second[part]
            push_p.wait_recv()
            add(whole_of(me[axis]), row0, rows, buf_p)
            push_m.wait_recv()
            add(whole_of(me[axis]), row0, rows, buf_m)
    out_v[...] = (mid[...].astype(f32) + total[me["x"], me["z"], me["y"]].astype(f32)).astype(bf16)
    done = pltpu.make_async_copy(out_v, out, local_sem.at[slots])
    done.start()
    done.wait()
    links.finish()


def row_sum(terms, mid):
    rows, cols = mid.shape
    n = 12 + 36
    bufs = []
    for phase in range(3):
        for (_, part_rows, half, _), order in zip(ROW_PARTS, SUM_ORDERS):
            open_dims = [d for d in SUM_DIMS if d in order[phase + 1 :]]
            rest = (RING,) * len(open_dims)
            if phase == 2:
                bufs += [(half, cols), (part_rows - half, cols)]
            else:
                bufs += [tuple(2 if d == order[phase + 1] else RING for d in open_dims) + (part_rows, cols)] * 2
            bufs += [rest + (part_rows, cols)] * 2

    def kernel(terms, mid, out, total, other, *rest):
        row_sum_kernel(terms, mid, out, total, other, rest[:36], *rest[36:])

    return pl.pallas_call(
        kernel,
        out_shape=jax.ShapeDtypeStruct((rows, cols), bf16),
        in_specs=[ANY, WHOLE],
        out_specs=ANY,
        scratch_shapes=[
            pltpu.VMEM((RING, RING, RING, rows, cols), bf16),
            pltpu.VMEM((RING, RING, RING, rows, cols), bf16),
        ]
        + [pltpu.VMEM(shape, bf16) for shape in bufs]
        + [
            pltpu.VMEM((rows, cols), bf16),
            pltpu.SemaphoreType.DMA((n,)),
            pltpu.SemaphoreType.DMA((n,)),
            pltpu.SemaphoreType.DMA((13,)),
        ],
        compiler_params=pltpu.CompilerParams(
            collective_id=3, has_side_effects=True, vmem_limit_bytes=48 << 20
        ),
        name="row_sum",
    )(terms, mid)


def attend_kernel(where, pages, queries, first, gathered, out, cache, window, zeros, sems):
    span = window.shape[0]
    block = where[0]
    start = where[1]
    slots = cache.shape[0]
    grab = pltpu.make_async_copy(gathered.at[pl.ds(start, span)], window, sems.at[0])
    grab.start()
    zeros[...] = jnp.zeros_like(zeros)

    def page_copy(slot, page):
        return pltpu.make_async_copy(
            gathered.at[page // 8, pl.ds(pl.multiple_of(lax.rem(page, 8) * PAGE, PAGE), PAGE), :],
            cache.at[slot],
            sems.at[1 + slot],
        )

    def empty_copy(slot):
        return pltpu.make_async_copy(zeros, cache.at[slot], sems.at[1 + slot])

    def send(slot, carry):
        page = pages[slot]

        @pl.when(page >= 0)
        def _():
            page_copy(slot, page).start()

        @pl.when(page < 0)
        def _():
            empty_copy(slot).start()

        return carry

    lax.fori_loop(0, slots, send, 0)
    grab.wait()
    rows = queries.shape[0]
    width = span * rows
    held = window[...][:, :rows, :]
    keys = held[:, :, :HEAD_DIM].reshape(width, HEAD_DIM)
    values = held[:, :, HEAD_DIM:].reshape(width, HEAD_DIM)
    key_at = start * rows + lax.broadcasted_iota(jnp.int32, (rows, width), 1)
    query_at = block * rows + lax.broadcasted_iota(jnp.int32, (rows, width), 0)
    allowed = (key_at <= query_at) & (key_at >= first[...])
    for head in range(queries.shape[1] // HEAD_DIM):
        cols = pl.ds(head * HEAD_DIM, HEAD_DIM)
        scores = lax.dot_general(
            queries[:, cols], keys, (((1,), (1,)), ((), ())), preferred_element_type=f32
        ) * (HEAD_DIM**-0.5)
        scores = jnp.where(allowed, scores, masked_score)
        weights = jnp.where(allowed, jnp.exp(scores - jnp.max(scores, axis=1, keepdims=True)), 0.0)
        totals = jnp.sum(weights, axis=1, keepdims=True)
        mixed = jnp.dot(weights.astype(bf16), values, preferred_element_type=f32)
        out[:, cols] = (mixed / totals).astype(bf16)

    def settle(slot, carry):
        empty_copy(slot).wait()
        return carry

    lax.fori_loop(0, slots, settle, 0)


def attend(block, pages, queries, first, gathered):
    blocks = gathered.shape[0]
    span = min(9, blocks)
    start = jnp.clip(block - 8, 0, blocks - span)
    width = gathered.shape[2]
    return pl.pallas_call(
        attend_kernel,
        grid_spec=pltpu.PrefetchScalarGridSpec(
            num_scalar_prefetch=2,
            grid=(1,),
            in_specs=[
                pl.BlockSpec(queries.shape, lambda i, *_: (0, 0)),
                pl.BlockSpec(first.shape, lambda i, *_: (0, 0)),
                ANY,
            ],
            out_specs=(pl.BlockSpec(queries.shape, lambda i, *_: (0, 0)), ANY),
            scratch_shapes=[
                pltpu.VMEM((span,) + gathered.shape[1:], bf16),
                pltpu.VMEM((PAGE, width), bf16),
                pltpu.SemaphoreType.DMA((1 + pages.shape[0],)),
            ],
        ),
        out_shape=(
            jax.ShapeDtypeStruct(queries.shape, bf16),
            jax.ShapeDtypeStruct((pages.shape[0], PAGE, width), bf16),
        ),
        compiler_params=pltpu.CompilerParams(vmem_limit_bytes=32 << 20),
        name="attend",
    )(jnp.stack([block, start]).astype(jnp.int32), pages, queries, first, gathered)


GROUP = 8
PAIR = 2


def expert_kernel(slot_row, slot_col, gates, rows, w_gate, w_up, w_down, out, packed, made):
    tokens = rows.shape[2]
    pair_cap = PAIR * CAP
    n_exp = w_gate.shape[0]
    quarter = rows.shape[3]
    gate_of = []
    for p in range(GROUP // PAIR):
        picks = []
        for e in range(n_exp):
            lane = slot_row[p, e : e + 1, :]
            row = lax.broadcasted_iota(jnp.int32, (pair_cap, PAIR * tokens), 0)
            picks.append(jnp.broadcast_to(lane, row.shape) == row)
        pick = jnp.concatenate(picks, axis=0)
        weight = jnp.concatenate(
            [jnp.broadcast_to(gates[p, e : e + 1, :], (pair_cap, PAIR * tokens)) for e in range(n_exp)], axis=0
        )
        gate_of.append(jnp.sum(jnp.where(pick, weight, 0.0), axis=1, keepdims=True))
        pick = pick.astype(f32).astype(bf16)
        for q in range(RING):
            block = rows[PAIR * p : PAIR * p + PAIR, q].reshape(PAIR * tokens, quarter)
            got = jnp.dot(pick, block, preferred_element_type=f32).astype(bf16)
            for e in range(n_exp):
                packed[e, p * pair_cap : (p + 1) * pair_cap, q * quarter : (q + 1) * quarter] = got[
                    e * pair_cap : (e + 1) * pair_cap
                ]
    for e in range(n_exp):
        x = packed[e]
        gate_term = jnp.dot(x, w_gate[e], preferred_element_type=f32)
        up_term = jnp.dot(x, w_up[e], preferred_element_type=f32)
        act = (gate_term / (1.0 + jnp.exp(-gate_term)) * up_term).astype(bf16)
        scale = jnp.concatenate(
            [gate_of[p][e * pair_cap : (e + 1) * pair_cap] for p in range(GROUP // PAIR)], axis=0
        )
        for q in range(RING):
            down = jnp.dot(act, w_down[e][:, q * quarter : (q + 1) * quarter], preferred_element_type=f32)
            down = (down * scale).astype(bf16)
            for p in range(GROUP // PAIR):
                made[p, e * pair_cap : (e + 1) * pair_cap, q * quarter : (q + 1) * quarter] = down[
                    p * pair_cap : (p + 1) * pair_cap
                ]
    for p in range(GROUP // PAIR):
        spread = []
        for e in range(n_exp):
            col = slot_col[p, :, e : e + 1]
            lane = lax.broadcasted_iota(jnp.int32, (PAIR * tokens, pair_cap), 1)
            spread.append((jnp.broadcast_to(col, lane.shape) == lane).astype(f32))
        spread = jnp.concatenate(spread, axis=1).astype(bf16)
        for q in range(RING):
            back = jnp.dot(spread, made[p, :, q * quarter : (q + 1) * quarter], preferred_element_type=f32)
            out[PAIR * p : PAIR * p + PAIR, q] = back.astype(bf16).reshape(PAIR, tokens, quarter)


def experts(slot_row, slot_col, gates, rows, w_gate, w_up, w_down):
    blocks, _, tokens, quarter = rows.shape
    n_exp, width, ff = w_gate.shape
    pairs = GROUP // PAIR
    pair_cap = PAIR * CAP

    def fixed(shape):
        return pl.BlockSpec(shape, lambda i: (0,) * len(shape), pipeline_mode=pl.Buffered(1))

    return pl.pallas_call(
        expert_kernel,
        grid=(blocks // GROUP,),
        in_specs=[
            pl.BlockSpec((pairs, n_exp, PAIR * tokens), lambda i: (i, 0, 0)),
            pl.BlockSpec((pairs, PAIR * tokens, n_exp), lambda i: (i, 0, 0)),
            pl.BlockSpec((pairs, n_exp, PAIR * tokens), lambda i: (i, 0, 0)),
            pl.BlockSpec((GROUP, RING, tokens, quarter), lambda i: (i, 0, 0, 0)),
            fixed(w_gate.shape),
            fixed(w_up.shape),
            fixed(w_down.shape),
        ],
        out_specs=pl.BlockSpec((GROUP, RING, tokens, quarter), lambda i: (i, 0, 0, 0)),
        out_shape=jax.ShapeDtypeStruct(rows.shape, bf16),
        scratch_shapes=[
            pltpu.VMEM((n_exp, GROUP * CAP, width), bf16),
            pltpu.VMEM((pairs, n_exp * pair_cap, width), bf16),
        ],
        compiler_params=pltpu.CompilerParams(vmem_limit_bytes=56 << 20),
        name="experts",
    )(slot_row, slot_col, gates, rows, w_gate, w_up, w_down)


def rms_norm(values, gain_vec):
    widened = values.astype(f32)
    factor = lax.rsqrt(jnp.mean(widened * widened, axis=-1, keepdims=True) + epsilon)
    return (widened * factor * gain_vec).astype(bf16)


def rotate(values, position):
    half_dim = HEAD_DIM // 2
    inverse = rope_base ** (-2.0 * jnp.arange(half_dim, dtype=f32) / HEAD_DIM)
    angles = position.astype(f32)[:, None] * inverse[None, :]
    cosine, sine = jnp.cos(angles), jnp.sin(angles)
    heads = []
    for head in range(values.shape[1] // HEAD_DIM):
        one = values[:, head * HEAD_DIM : (head + 1) * HEAD_DIM]
        first, second = one[:, :half_dim], one[:, half_dim:]
        heads += [first * cosine - second * sine, second * cosine + first * sine]
    return jnp.concatenate(heads, axis=1).astype(bf16)


def segment_start(seg_lengths, positions):
    count = seg_lengths.shape[0]
    earlier = jnp.arange(count)[None, :] < jnp.arange(count)[:, None]
    starts = jnp.sum(jnp.where(earlier, seg_lengths[None, :], 0), axis=1)
    return jnp.max(jnp.where(starts[None, :] <= positions[:, None], starts[None, :], 0), axis=1)


def local(
    hidden, gain_attn, w_query, w_key, w_value, w_out, gain_moe, expert_ids, expert_gates,
    w_gate, w_up, w_down, seg_lengths, slot_page,
):
    tok_rows, model_width = hidden.shape
    shard_count = lax.axis_size("seq")
    shard_index = lax.axis_index("seq")
    tensor_index = lax.axis_index("tp")
    quarter = model_width // RING
    positions = shard_index * tok_rows + jnp.arange(tok_rows, dtype=jnp.int32)
    seg_first = segment_start(seg_lengths, positions)
    offsets = positions - seg_first
    normed = rms_norm(hidden, gain_attn)
    queries = rotate(jnp.dot(normed, w_query, preferred_element_type=f32), offsets)
    keys_rot = rotate(jnp.dot(normed, w_key, preferred_element_type=f32), offsets)
    values = jnp.dot(normed, w_value, preferred_element_type=f32).astype(bf16)
    gate_high = expert_gates.astype(bf16)
    gate_low = (expert_gates - gate_high.astype(f32)).astype(bf16)
    routing = jnp.concatenate([expert_ids.astype(bf16), gate_high, gate_low], axis=1).T
    routing = jnp.pad(routing.reshape(3 * TOP * tok_rows // 256, 256), ((0, 7), (0, 0)))
    sent = jnp.concatenate([jnp.concatenate([keys_rot, values], axis=1), routing], axis=0)
    gathered = kv_gather(sent).reshape(shard_count, tok_rows + 16, 256)
    slot_count = slot_page.shape[0] // shard_count
    own_slots = lax.dynamic_slice_in_dim(slot_page, shard_index * slot_count, slot_count)
    attended, kv_cache = attend(shard_index, own_slots, queries, seg_first[:, None], gathered)
    table = gathered[:, tok_rows : tok_rows + 9, :].reshape(shard_count, 3 * TOP, tok_rows).astype(f32)
    n_exp = w_gate.shape[0]
    mine = shard_index * n_exp + jnp.arange(n_exp)
    hits = table[:, None, :TOP, :] == mine[None, :, None, None].astype(f32)
    gates = jnp.sum(
        jnp.where(hits, table[:, None, TOP : 2 * TOP, :] + table[:, None, 2 * TOP :, :], 0.0), axis=2
    )
    named = jnp.any(hits, axis=2)
    before = (jnp.arange(tok_rows)[:, None] < jnp.arange(tok_rows)[None, :]).astype(bf16)
    rank = jnp.einsum("set,tu->seu", named.astype(bf16), before, preferred_element_type=f32)
    pair_at = (jnp.arange(shard_count) % PAIR * CAP)[:, None, None]
    slot = jnp.where(named, rank.astype(jnp.int32) + pair_at, -1)

    def paired(values):
        return values.reshape(shard_count // PAIR, PAIR, n_exp, tok_rows).swapaxes(1, 2).reshape(
            shard_count // PAIR, n_exp, PAIR * tok_rows
        )

    slot_row, gates = paired(slot), paired(gates)
    slot_col = slot_row.swapaxes(1, 2)
    terms = jnp.stack(
        [
            jnp.dot(attended, w_out[:, q * quarter : (q + 1) * quarter], preferred_element_type=f32)
            for q in range(RING)
        ]
    ).astype(bf16)
    own_hidden = lax.dynamic_slice_in_dim(hidden, tensor_index * quarter, quarter, 1)
    own_gain = lax.dynamic_slice_in_dim(gain_moe, tensor_index * quarter, quarter)[None, :]
    rows, mid = row_gather(terms, own_hidden, own_gain)
    made = experts(
        slot_row, slot_col, gates, rows.reshape(shard_count, RING, tok_rows, quarter), w_gate, w_up, w_down
    )
    return (row_sum(made.reshape(rows.shape), mid), kv_cache)


def solution(mesh):
    placed = (
        P("seq", None),
        P(),
        P(None, "tp"),
        P(None, "tp"),
        P(None, "tp"),
        P("tp", None),
        P(),
        P("seq", None),
        P("seq", None),
        P("seq", None, "tp"),
        P("seq", None, "tp"),
        P("seq", "tp", None),
        P(),
        P(),
    )
    return jax.shard_map(
        local,
        mesh=mesh,
        in_specs=placed,
        out_specs=(P("seq", "tp"), P("seq", None, "tp")),
        check_vma=False,
    )
```

time: 598 us -> 239 us (0.40)
  Pallas kernels: 0 us -> 204 us
  local copies, waits for them, and re-layouts: 195 us -> 14.9 us
  waiting for transfers between devices: 180 us -> 0 us
  blocking collectives: 97.1 us -> 0 us
  matrix products: 59.8 us -> 11.8 us
  other arithmetic: 37.6 us -> 6.81 us
  between operations: 14.1 us -> 0.89 us
  starting transfers between devices: 7.5 us -> 0 us
    pallas_call x0 -> x5, Pallas kernels: none -> 204 us  [the longest x1 76.3 us: row_gather(): pl.pallas_call(row_gather_kernel, out_shape=(jax.ShapeDtypeStruct((RING,...]
    unnamed x36 -> x15, local copies, waits for them, and re-layouts: 124 us -> 9.33 us
    all_to_all x1 -> x0, blocking collectives: 97.1 us -> none  [local(): lax.all_to_all(packed.reshape(shard_count, exp_local, capacity, moe_in.sh...]
    unnamed x4 -> x0, waiting for transfers between devices: 74.6 us -> none
    dot_general x32 -> x8, matrix products: 59.8 us -> 11.8 us  [the longest x4 5.87 us: local(): jnp.dot(attended, w_out[:, q * quarter:(q + 1) * quarter], preferred_elem...]
    all_gather x1 -> x0, waiting for transfers between devices: 40 us -> none  [local(): portion = lax.all_gather(kv_rows, 'seq', axis=0, tiled=True)]
    psum x1 -> x0, waiting for transfers between devices: 39.6 us -> none  [local(): lax.psum(partial_value.astype(jnp.bfloat16), 'tp').astype(jnp.float32)]
    all_to_all x1 -> x0, waiting for transfers between devices: 26 us -> none  [local(): lax.all_to_all(merged, 'seq', split_axis=0, concat_axis=0, tiled=True)]
  transfers between devices with their start and end apart: 4 -> 0, of which waited for: 4 -> 0; matrix products, arithmetic and copies ran while one was open for 2% -> 0% of each run, Pallas kernels for 0% -> 0%
where the time goes in v1:
time: 239 us; the launch traced here: 238 us
  Pallas kernels  204 us (85%)
  local copies, waits for them, and re-layouts  14.9 us (6%)
  matrix products  11.8 us (5%)
  other arithmetic  6.81 us (3%)
    pallas_call x1, Pallas kernels, row_gather(): pl.pallas_call(row_gather_kernel, out_shape=(jax.ShapeDtypeStruct((RING,...  76.3 us
    pallas_call x1, Pallas kernels, row_sum(): pl.pallas_call(kernel, out_shape=jax.ShapeDtypeStruct((rows, cols), bf16)...  66.8 us
    pallas_call x1, Pallas kernels, experts(): pl.pallas_call(expert_kernel, grid=(blocks // GROUP,), in_specs=[pl.Block...  32 us
    pallas_call x1, Pallas kernels, kv_gather(): pl.pallas_call(kv_gather_kernel, out_shape=jax.ShapeDtypeStruct((RING, RI...  23.6 us
    unnamed x15, local copies, waits for them, and re-layouts  9.33 us
    dot_general x4, matrix products, local(): jnp.dot(attended, w_out[:, q * quarter:(q + 1) * quarter], preferred_elem...  5.87 us
    pallas_call x1, Pallas kernels, attend(): pl.pallas_call(attend_kernel, grid_spec=pltpu.PrefetchScalarGridSpec(num_...  5.15 us

profile of v1, /device:TPU:0, one launch (start us, length us, event | category | flops | bytes accessed | tf_op | source)
XLA Modules:
  0.0 238.2 jit_solution(1543349671856739963)
XLA Ops:
  0.8 0.9 dynamic_slice.9.pages
  1.7 0.8 select_reduce_fusion.1
  2.5 1.3 fusion
  4.4 0.7 convert_element_type.57
  5.1 0.8 dynamic_slice.11
  5.9 0.8 subtract_convert_fusion
  6.6 2.3 convolution_convert_fusion.4
  9.1 1.7 fusion.70
  10.7 0.9 constant_dynamic-slice_fusion.hidden
  11.7 1.8 fusion.67
  14.4 1.5 fusion.39.src
  15.9 23.6 %kv_gather.1 = bf16[4,4,2,144,256]{4,3,2,1,0:T(8,128)(2,1)} custom-call(bf16[144,256]{1,0:T(8,128)(2,1)} %fusion.39.src), custom_call_target="tpu_custom_call" | custom-call | tf_op jit(solution)/shard_map/kv_gather/pallas_call | solution.py:151
  39.5 1.7 copy-done.3
  41.2 5.2 %attend.1 = (bf16[128,640]{1,0:T(8,128)(2,1)S(1)}, bf16[64,16,256]{2,1,0:T(8,128)(2,1)}) custom-call(s32[2]{0:T(128)S(1)} %pad_add_fusion.where, s32[64]{0:T(128)S(1)} %dynamic_slice.9.pages, bf16[128,640]{1,0:T(8,128)(2,1)S(1)} %concatenate.19.queries, s32[128,1]{1,0:T(8,128)S(1)} %copy.46.first, bf16[32,144,256]{2,1,0:T(8,128)(2,1)S(1)} %bitcast.39), custom_call_target="tpu_custom_call" | custom-call | tf_op jit(solution)/shard_map/attend/pallas_call | solution.py:463
  47.5 1.5 fusion.6
  49.0 1.5 fusion.5
  50.5 1.5 fusion.4
  51.9 1.5 fusion.3
  54.2 1.3 copy.47.slot_row
  55.5 76.3 %row_gather.1 = (bf16[4,4,2,4,128,640]{5,4,3,2,1,0:T(8,128)(2,1)S(1)}, bf16[128,640]{1,0:T(8,128)(2,1)S(1)}) custom-call(bf16[4,128,640]{2,1,0:T(8,128)(2,1)S(1)} %pad_maximum_fusion.terms, bf16[128,640]{1,0:T(8,128)(2,1)S(1)} %constant_dynamic-slice_fusion.hidden, f32[1,640]{1,0:T(1,128)S(1)} %broadcast_in_dim.46.gain), custom_call_target="tpu_custom_call" | custom-call | tf_op jit(solution)/shard_map/row_gather/pallas_call | solution.py:204
  131.8 7.0 %copy-done.2 = bf16[4,4,2,4,128,640]{5,4,3,2,1,0:T(8,128)(2,1)} copy-done((bf16[4,4,2,4,128,640]{5,4,3,2,1,0:T(8,128)(2,1)}, bf16[4,4,2,4,128,640]{5,4,3,2,1,0:T(8,128)(2,1)S(1)}, u32[]{:S(2)}) %copy-start.2) | copy-done | bytes 20971544
  138.8 32.0 %experts.1 = bf16[32,4,128,640]{3,2,1,0:T(8,128)(2,1)} custom-call(s32[16,2,256]{2,1,0:T(2,128)} %copy.47.slot_row, s32[16,256,2]{2,1,0:T(8,128)} %bitcast.43, f32[16,2,256]{2,1,0:T(2,128)} %copy.50.gates, bf16[32,4,128,640]{3,2,1,0:T(8,128)(2,1)} %bitcast.38, bf16[2,2560,384]{2,1,0:T(8,128)(2,1)} %w_gate.1, bf16[2,2560,384]{2,1,0:T(8,128)(2,1)} %w_up.1, ...), custom_call_target="tpu_custom_call" | custom-call | tf_op jit(solution)/shard_map/experts/pallas_call | solution.py:554
  170.8 66.8 %row_sum.1 = bf16[128,640]{1,0:T(8,128)(2,1)S(1)} custom-call(bf16[4,4,2,4,128,640]{5,4,3,2,1,0:T(8,128)(2,1)} %bitcast.41, bf16[128,640]{1,0:T(8,128)(2,1)S(1)} %get-tuple-element.8.mid), custom_call_target="tpu_custom_call" | custom-call | tf_op jit(solution)/shard_map/row_sum/pallas_call | solution.py:375
  237.6 0.7 copy.52
  (39 shorter events, 3.6 us)
Async XLA Ops:
  0.6 11.1 %copy-start = (bf16[2560,640]{1,0:T(8,128)(2,1)S(1)}, bf16[2560,640]{1,0:T(8,128)(2,1)}, u32[]{:S(2)}) copy-start(bf16[2560,640]{1,0:T(8,128)(2,1)} %param.16) | copy-start | bytes 9830404
  0.6 8.4 %copy-start.5 = (f32[2560]{0:T(1024)S(1)}, f32[2560]{0:T(1024)}, u32[]{:S(2)}) copy-start(f32[2560]{0:T(1024)} %param.15) | copy-start | bytes 30724
  39.5 1.7 copy-start.3
  41.2 6.2 %copy-start.6 = (s32[32]{0:T(128)S(1)}, s32[32]{0:T(128)}, u32[]{:S(2)}) copy-start(s32[32]{0:T(128)} %fusion.66) | copy-start | bytes 388
  54.1 84.6 %copy-start.4 = (s32[16,2,2,128]{2,3,1,0:T(8,128)}, s32[16,2,2,128]{2,3,1,0:T(8,128)S(1)}, u32[]{:S(2)}) copy-start(s32[16,2,2,128]{2,3,1,0:T(8,128)S(1)} %copy.43) | copy-start | bytes 98308
  131.8 7.0 %copy-start.2 = (bf16[4,4,2,4,128,640]{5,4,3,2,1,0:T(8,128)(2,1)}, bf16[4,4,2,4,128,640]{5,4,3,2,1,0:T(8,128)(2,1)S(1)}, u32[]{:S(2)}) copy-start(bf16[4,4,2,4,128,640]{5,4,3,2,1,0:T(8,128)(2,1)S(1)} %get-tuple-element.7) | copy-start | bytes 62914564
  170.8 67.5 %copy-start.1 = (bf16[2560,640]{1,0:T(8,128)(2,1)S(1)}, bf16[2560,640]{1,0:T(8,128)(2,1)}, u32[]{:S(2)}) copy-start(bf16[2560,640]{1,0:T(8,128)(2,1)} %param.16) | copy-start | bytes 9830404

commit v2 on v1

v2 whole, which is shorter than its diff:
```python
import functools

import jax
import jax.numpy as jnp
from jax import lax
from jax.experimental import pallas as pl
from jax.experimental.pallas import tpu as pltpu
from jax.sharding import PartitionSpec as P

HEAD_DIM = 128
TOP = 6
PAGE = 16
CAP = 24
RING = 4
MESH = pl.DeviceIdType.MESH
ANY = pl.BlockSpec(memory_space=pl.ANY)
WHOLE = pl.BlockSpec(memory_space=pltpu.VMEM)
epsilon = 1e-05
rope_base = 500000.0
masked_score = -1e30
bf16 = jnp.bfloat16
f32 = jnp.float32


def my_place():
    index = lax.axis_index("seq")
    return {
        "x": index // 8,
        "z": lax.rem(index // 2, RING),
        "c": lax.rem(index, 2),
        "y": lax.axis_index("tp"),
    }


def device_at(place):
    return ((place["x"] * RING + place["z"]) * 2 + place["c"], place["y"])


def moved(place, axis, step):
    size = 2 if axis == "c" else RING
    other = dict(place)
    other[axis] = lax.rem(place[axis] + step + size, size)
    return other


def enter(places):
    barrier = pltpu.get_barrier_semaphore()
    for place in places:
        pl.semaphore_signal(barrier, inc=1, device_id=device_at(place), device_id_type=MESH)
    pl.semaphore_wait(barrier, len(places))


class Links:
    def __init__(self, send_sem, recv_sem):
        self.send_sem, self.recv_sem, self.count = send_sem, recv_sem, 0
        self.started = []

    def push(self, src, dst, place):
        copy = pltpu.make_async_remote_copy(
            src_ref=src,
            dst_ref=dst,
            send_sem=self.send_sem.at[self.count],
            recv_sem=self.recv_sem.at[self.count],
            device_id=device_at(place),
            device_id_type=MESH,
        )
        self.count += 1
        copy.start()
        self.started.append(copy)
        return copy

    def finish(self):
        for copy in self.started:
            copy.wait_send()


def torus_gather(me, dims, parts, src, out, links, local_sem, beside=None):
    sibling = moved(me, "c", 1)

    def at(where, row0, rows):
        return out.at[tuple(where[d] for d in dims) + (pl.ds(row0, rows), slice(None))]

    own = {d: me[d] for d in dims}
    local = pltpu.make_async_copy(src, at(own, 0, src.shape[0]), local_sem)
    local.start()
    to_sibling = [links.push(src, at(own, 0, src.shape[0]), sibling)]
    for phase in range(len(parts[0][3])):
        if phase == 1:
            local.wait()
        live = []
        for row0, rows, half, order in parts:
            axis = order[phase]
            base = dict(own)
            for done in order[:phase]:
                base[done] = slice(None)
            whole = at(base, row0, rows)
            source = src.at[pl.ds(row0, rows), :] if phase == 0 else whole
            up = links.push(source, whole, moved(me, axis, 1))
            down = links.push(source, whole, moved(me, axis, -1))
            live.append((row0, rows, half, order, axis, base, up, down))
        if phase == 0 and beside is not None:
            beside()
        forwarded = []
        for row0, rows, half, order, axis, base, up, down in live:
            for copy, step in ((up, 1), (down, -1)):
                copy.wait_recv()
                got = dict(base)
                got[axis] = moved(me, axis, -step)[axis]
                if phase == 0:
                    r0, rn = (row0, half) if step == 1 else (row0 + half, rows - half)
                    piece = at(got, r0, rn)
                else:
                    cut = dict(got)
                    cut[order[0]] = pl.ds(0, 2) if step == 1 else pl.ds(2, 2)
                    piece = at(cut, row0, rows)
                forwarded.append(links.push(piece, piece, moved(me, axis, step)))
                there = at(got, row0, rows)
                to_sibling.append(links.push(there, there, sibling))
        for n, (row0, rows, half, order, axis, base, up, down) in enumerate(live):
            forwarded[2 * n].wait_recv()
            forwarded[2 * n + 1].wait_recv()
            got = dict(base)
            got[axis] = moved(me, axis, 2)[axis]
            there = at(got, row0, rows)
            to_sibling.append(links.push(there, there, sibling))
    for copy in to_sibling:
        copy.wait_recv()


def copies_of_gather(parts):
    phases = len(parts[0][3])
    return 1 + phases * len(parts) * 7


KV_PARTS = ((0, 80, 48, ("x", "z")), (80, 64, 32, ("z", "x")))
UNIT = (16, 128)
ROW_PARTS = (
    (0, 14, ("z", "y", "x")),
    (14, 13, ("y", "x", "z")),
    (27, 13, ("x", "z", "y")),
)
STREAMS = ((0, 1), (1, -1), (-1, 1), (2, -1))


def wave(stages):
    for stage in range(stages):
        for n in range(len(STREAMS)):
            yield stage, n


def to_units(values):
    rows, cols = values.shape
    return [
        values[:, j * 128 : (j + 1) * 128].reshape(rows // 16, 16, 128) for j in range(cols // 128)
    ]


def from_units(units, rows):
    group = rows // 16
    tiles = [units[j * group : (j + 1) * group].reshape(rows, 128) for j in range(units.shape[0] // group)]
    return jnp.concatenate(tiles, axis=1)


def stream_gather(me, src, out, links, local_sem):
    sibling = moved(me, "c", 1)

    def at(where, first, count):
        return out.at[where["x"], where["z"], where["c"], where["y"], pl.ds(first, count)]

    local = pltpu.make_async_copy(src, at(me, 0, src.shape[0]), local_sem)
    local.start()
    echo = []
    landed = {}
    for p, (u0, n, order) in enumerate(ROW_PARTS):
        piece = src.at[pl.ds(u0, n)]
        for step in (1, -1, 2):
            landed[p, step] = links.push(piece, at(me, u0, n), moved(me, order[0], step))
    state = {}

    def region(p, stream, ring, step):
        u0, n, order = ROW_PARTS[p]
        where = dict(me)
        where[order[0]] = moved(me, order[0], STREAMS[stream][0])[order[0]]
        if ring == 2:
            where[order[1]] = slice(None)
        where[order[ring]] = moved(me, order[ring], step)[order[ring]]
        return at(where, u0, n)

    def relay(ref):
        echo.append(links.push(ref, ref, sibling))

    for stage, stream in wave(6):
        step, way = STREAMS[stream]
        for p, (u0, n, order) in enumerate(ROW_PARTS):
            ring = 1 + stage // 3
            axis = order[ring]
            if stage % 3 == 0:
                if stage == 0:
                    if step == 0:
                        if p == 0:
                            local.wait()
                    else:
                        landed[p, -step if step != 2 else 2].wait_recv()
                else:
                    state[p, stream, 1, "far"].wait_recv()
                    whole = dict(me)
                    whole[order[0]] = moved(me, order[0], step)[order[0]]
                    whole[order[1]] = slice(None)
                    relay(at(whole, u0, n))
                own = region(p, stream, ring, 0)
                for w in (1, -1):
                    state[p, stream, ring, w] = links.push(own, own, moved(me, axis, w))
            elif stage % 3 == 1:
                state[p, stream, ring, way].wait_recv()
                near = region(p, stream, ring, -way)
                state[p, stream, ring, "far"] = links.push(near, near, moved(me, axis, way))
                state[p, stream, ring, -way].wait_recv()
                if ring == 2:
                    relay(near)
                    relay(region(p, stream, ring, way))
            elif ring == 2:
                state[p, stream, ring, "far"].wait_recv()
                relay(region(p, stream, ring, 2))
    for copy in echo:
        copy.wait_recv()


STREAM_COPIES = len(ROW_PARTS) * (3 + 4 * (3 + 4 + 3))


def turn(one, cosine, sine):
    return one * cosine + pltpu.roll(one, HEAD_DIM // 2, 1) * sine


def front_kernel(
    lengths, hidden, gain, inverse, routing, w_query, w_key, w_value,
    gathered, queries, first, sent, wq, wk, wv, normed, send_sem, recv_sem, local_sem,
):
    me = my_place()
    loads = [
        pltpu.make_async_copy(src, dst, local_sem.at[1 + n])
        for n, (src, dst) in enumerate(((w_key, wk), (w_value, wv), (w_query, wq)))
    ]
    for load in loads:
        load.start()
    rows = hidden.shape[0]
    block = (me["x"] * RING + me["z"]) * 2 + me["c"]
    at = block * rows + lax.broadcasted_iota(jnp.int32, (rows, 1), 0)
    begin = jnp.zeros((rows, 1), jnp.int32)
    running = lengths[0]
    for n in range(1, lengths.shape[0]):
        begin = jnp.where(at >= running, running, begin)
        running = running + lengths[n]
    first[...] = begin
    angles = (at - begin).astype(f32) * inverse[...]
    cosine = jnp.cos(angles)
    lane = lax.broadcasted_iota(jnp.int32, angles.shape, 1)
    sine = jnp.where(lane < HEAD_DIM // 2, -jnp.sin(angles), jnp.sin(angles))
    wide = hidden[...].astype(f32)
    factor = lax.rsqrt(jnp.mean(wide * wide, axis=1, keepdims=True) + epsilon)
    normed[...] = (wide * factor * gain[...]).astype(bf16)
    turned = routing[...].T
    sent[rows : rows + 16, :HEAD_DIM] = turned[:16].astype(bf16)
    sent[rows : rows + 16, HEAD_DIM:] = turned[16:32].astype(bf16)
    loads[0].wait()
    key = jnp.dot(normed[...], wk[...], preferred_element_type=f32)
    sent[:rows, :HEAD_DIM] = turn(key, cosine, sine).astype(bf16)
    loads[1].wait()
    sent[:rows, HEAD_DIM:] = jnp.dot(normed[...], wv[...], preferred_element_type=f32).astype(bf16)
    enter([moved(me, a, s) for a in ("x", "z") for s in (1, -1)] + [moved(me, "c", 1)])
    links = Links(send_sem, recv_sem)

    def beside():
        loads[2].wait()
        raw = jnp.dot(normed[...], wq[...], preferred_element_type=f32)
        for head in range(raw.shape[1] // HEAD_DIM):
            cols = slice(head * HEAD_DIM, (head + 1) * HEAD_DIM)
            queries[:, cols] = turn(raw[:, cols], cosine, sine).astype(bf16)

    torus_gather(me, ("x", "z", "c"), KV_PARTS, sent, gathered, links, local_sem.at[0], beside)
    links.finish()


def front(lengths, hidden, gain, inverse, routing, w_query, w_key, w_value):
    n = copies_of_gather(KV_PARTS)
    rows = hidden.shape[0]
    width = w_key.shape[1] + w_value.shape[1]
    return pl.pallas_call(
        front_kernel,
        out_shape=(
            jax.ShapeDtypeStruct((RING, RING, 2, rows + 16, width), bf16),
            jax.ShapeDtypeStruct((rows, w_query.shape[1]), bf16),
            jax.ShapeDtypeStruct((rows, 1), jnp.int32),
        ),
        in_specs=[pl.BlockSpec(memory_space=pltpu.SMEM)] + [WHOLE] * 4 + [ANY] * 3,
        out_specs=(ANY, WHOLE, WHOLE),
        scratch_shapes=[
            pltpu.VMEM((rows + 16, width), bf16),
            pltpu.VMEM(w_query.shape, bf16),
            pltpu.VMEM(w_key.shape, bf16),
            pltpu.VMEM(w_value.shape, bf16),
            pltpu.VMEM(hidden.shape, bf16),
            pltpu.SemaphoreType.DMA((n,)),
            pltpu.SemaphoreType.DMA((n,)),
            pltpu.SemaphoreType.DMA((4,)),
        ],
        compiler_params=pltpu.CompilerParams(
            collective_id=1, has_side_effects=True, vmem_limit_bytes=48 << 20
        ),
        name="front",
    )(lengths, hidden, gain, inverse, routing, w_query, w_key, w_value)


def row_gather_kernel(
    terms, hidden, gain, out, mid, heard, squares, mid_v, row_v, send_sem, recv_sem, local_sem
):
    me = my_place()
    width = mid.shape[1]
    mine = pl.ds(pl.multiple_of(me["y"] * width, 128), width)
    peers = [moved(me, "y", s) for s in (1, 2, 3)]
    enter([moved(me, a, s) for a in ("x", "z") for s in (1, -1, 2)] + [moved(me, "c", 1)] + peers)
    links = Links(send_sem, recv_sem)
    sent = [
        links.push(terms.at[peer["y"]], heard.at[n], peer) for n, peer in enumerate(peers)
    ]
    total = terms[me["y"]].astype(f32)
    for n in range(3):
        sent[n].wait_recv()
        total = total + heard[n].astype(f32)
    mid_now = (hidden[:, mine].astype(f32) + total).astype(bf16)
    mid_v[...] = mid_now
    wide = mid_now.astype(f32)
    ours = jnp.sum(wide * wide, axis=1, keepdims=True)
    squares[3] = jnp.broadcast_to(ours, (ours.shape[0], 128)).T[:8]
    told = [links.push(squares.at[3], squares.at[n], peer) for n, peer in enumerate(peers)]
    whole = squares[3]
    for n in range(3):
        told[n].wait_recv()
        whole = whole + squares[n]
    whole = jnp.broadcast_to(whole[:1], (128, 128)).T[:, :1]
    factor = lax.rsqrt(whole * (1.0 / (RING * wide.shape[1])) + epsilon)
    ready = (wide * factor * gain[:, mine]).astype(bf16)
    for j, tile in enumerate(to_units(ready)):
        row_v[j * tile.shape[0] : (j + 1) * tile.shape[0]] = tile
    keep = pltpu.make_async_copy(mid_v, mid, local_sem.at[1])
    keep.start()
    stream_gather(me, row_v, out, links, local_sem.at[0])
    keep.wait()
    links.finish()


def row_gather(terms, hidden, gain):
    n = 6 + STREAM_COPIES
    rows, cols = terms.shape[1:]
    units = rows * cols // (UNIT[0] * UNIT[1])
    return pl.pallas_call(
        row_gather_kernel,
        out_shape=(
            jax.ShapeDtypeStruct((RING, RING, 2, RING, units) + UNIT, bf16),
            jax.ShapeDtypeStruct((rows, cols), bf16),
        ),
        in_specs=[WHOLE, WHOLE, WHOLE],
        out_specs=(ANY, ANY),
        scratch_shapes=[
            pltpu.VMEM((3, rows, cols), bf16),
            pltpu.VMEM((4, 8, rows), f32),
            pltpu.VMEM((rows, cols), bf16),
            pltpu.VMEM((units,) + UNIT, bf16),
            pltpu.SemaphoreType.DMA((n,)),
            pltpu.SemaphoreType.DMA((n,)),
            pltpu.SemaphoreType.DMA((2,)),
        ],
        compiler_params=pltpu.CompilerParams(
            collective_id=2, has_side_effects=True, vmem_limit_bytes=48 << 20
        ),
        name="row_gather",
    )(terms, hidden, gain)


SUM_DIMS = ("x", "z", "y")
SUM_STREAMS = ((2, 1), (1, -1), (-1, 1), (0, -1))


def row_sum_kernel(terms, mid, out, total, other, bufs, out_v, send_sem, recv_sem, local_sem):
    me = my_place()
    sibling = moved(me, "c", 1)
    enter([moved(me, a, s) for a in ("x", "z", "y") for s in (1, -1, 2)] + [sibling])
    links = Links(send_sem, recv_sem)

    def held(ref, where, u0, n):
        return ref.at[tuple(where[d] for d in SUM_DIMS) + (pl.ds(u0, n),)]

    def place(p, stream, **free):
        order = ROW_PARTS[p][2]
        where = dict(me)
        where[order[0]] = moved(me, order[0], SUM_STREAMS[stream][0])[order[0]]
        where.update(free)
        return where

    first = {}
    for stream in range(4):
        for p, (u0, n, order) in enumerate(ROW_PARTS):
            where = place(p, stream, **{order[1]: slice(None), order[2]: slice(None)})
            slot = stream * 3 + p
            keep = pltpu.make_async_copy(
                terms.at[where["x"], where["z"], me["c"], where["y"], pl.ds(u0, n)],
                held(total, where, u0, n),
                local_sem.at[slot],
            )
            keep.start()
            push = links.push(
                terms.at[where["x"], where["z"], sibling["c"], where["y"], pl.ds(u0, n)],
                held(other, where, u0, n),
                sibling,
            )
            first[p, stream] = (keep, push)

    def add(where, u0, n, buf, lead):
        span = pl.ds(u0, n)
        if lead is None:
            index = tuple(where[d] for d in SUM_DIMS) + (span,)
            total[index] = total[index] + buf[...]
            return

        def one(k, carry):
            index = tuple(k if d == lead else where[d] for d in SUM_DIMS) + (span,)
            total[index] = total[index] + buf[k]
            return carry

        lax.fori_loop(0, RING, one, 0)

    state = {}
    for stage, stream in wave(6):
        step, way = SUM_STREAMS[stream]
        for p, (u0, n, order) in enumerate(ROW_PARTS):
            if stage == 0:
                keep, push = first[p, stream]
                keep.wait()
                push.wait_recv()
                where = place(p, stream)
                span = pl.ds(u0, n)

                def one(k, carry, where=where, span=span, order=order):
                    spot = {order[1]: k // RING, order[2]: lax.rem(k, RING)}
                    index = tuple(spot.get(d, where[d]) for d in SUM_DIMS) + (span,)
                    total[index] = total[index] + other[index]
                    return carry

                lax.fori_loop(0, RING * RING, one, 0)
            ring = 2 - stage // 3
            axis = order[ring]
            lead = order[1] if ring == 2 else None
            free = {order[1]: slice(None)} if ring == 2 else {}
            far, near, back = bufs[((2 - ring) * 4 + stream) * 3 + p]
            at = lambda s: place(p, stream, **free, **{axis: moved(me, axis, s)[axis]})
            if stage % 3 == 0:
                state[p, stream, ring, "far"] = links.push(held(total, at(2), u0, n), far, moved(me, axis, way))
                state[p, stream, ring, "back"] = links.push(held(total, at(-way), u0, n), back, moved(me, axis, -way))
            elif stage % 3 == 1:
                state[p, stream, ring, "far"].wait_recv()
                add(at(way), u0, n, far, lead)
                state[p, stream, ring, "near"] = links.push(held(total, at(way), u0, n), near, moved(me, axis, way))
            else:
                state[p, stream, ring, "back"].wait_recv()
                add(at(0), u0, n, back, lead)
                state[p, stream, ring, "near"].wait_recv()
                add(at(0), u0, n, near, lead)
                if ring == 1 and step != 0:
                    state[p, stream, "last"] = links.push(
                        held(total, place(p, stream), u0, n), bufs[24 + stream * 3 + p][0], moved(me, order[0], step)
                    )
    for stream in range(3):
        for p, (u0, n, order) in enumerate(ROW_PARTS):
            state[p, stream, "last"].wait_recv()
            add(me, u0, n, bufs[24 + stream * 3 + p][0], None)
    done = from_units(total[me["x"], me["z"], me["y"]], out.shape[0])
    out_v[...] = (mid[...].astype(f32) + done.astype(f32)).astype(bf16)
    write = pltpu.make_async_copy(out_v, out, local_sem.at[12])
    write.start()
    write.wait()
    links.finish()


def row_sum(terms, mid):
    rows, cols = mid.shape
    units = terms.shape[4]
    n = 12 + 3 * (4 * 6 + 3)
    bufs = []
    for ring in (2, 1):
        for stream in range(4):
            for _, count, _ in ROW_PARTS:
                bufs += [((RING,) if ring == 2 else ()) + (count,) + UNIT] * 3
    for stream in range(3):
        for _, count, _ in ROW_PARTS:
            bufs += [(count,) + UNIT]

    def kernel(terms, mid, out, total, other, *rest):
        flat, rest = rest[: len(bufs)], rest[len(bufs) :]
        sets = [flat[3 * k : 3 * k + 3] for k in range(24)] + [flat[72 + k : 73 + k] for k in range(9)]
        row_sum_kernel(terms, mid, out, total, other, sets, *rest)

    return pl.pallas_call(
        kernel,
        out_shape=jax.ShapeDtypeStruct((rows, cols), bf16),
        in_specs=[ANY, WHOLE],
        out_specs=ANY,
        scratch_shapes=[
            pltpu.VMEM((RING, RING, RING, units) + UNIT, bf16),
            pltpu.VMEM((RING, RING, RING, units) + UNIT, bf16),
        ]
        + [pltpu.VMEM(shape, bf16) for shape in bufs]
        + [
            pltpu.VMEM((rows, cols), bf16),
            pltpu.SemaphoreType.DMA((n,)),
            pltpu.SemaphoreType.DMA((n,)),
            pltpu.SemaphoreType.DMA((13,)),
        ],
        compiler_params=pltpu.CompilerParams(
            collective_id=3, has_side_effects=True, vmem_limit_bytes=48 << 20
        ),
        name="row_sum",
    )(terms, mid)


def attend_kernel(
    where, pages, queries, first, gathered, w_out, terms, cache, slot, gates,
    window, meta, wo, zeros, attended, sems, page_sems,
):
    span = window.shape[0]
    block, start = where[0], where[1]
    slots = cache.shape[0]
    rows = queries.shape[0]
    grab = pltpu.make_async_copy(gathered.at[pl.ds(start, span)], window, sems.at[0])
    grab.start()
    note = pltpu.make_async_copy(gathered.at[:, pl.ds(rows, 16), :], meta, sems.at[1])
    note.start()
    load = pltpu.make_async_copy(w_out, wo, sems.at[2])
    load.start()
    zeros[...] = jnp.zeros_like(zeros)

    def page_copy(n, page):
        return pltpu.make_async_copy(
            gathered.at[page // 8, pl.ds(pl.multiple_of(lax.rem(page, 8) * PAGE, PAGE), PAGE), :],
            cache.at[n],
            page_sems.at[n],
        )

    def empty_copy(n):
        return pltpu.make_async_copy(zeros, cache.at[n], page_sems.at[n])

    def send(n, carry):
        page = pages[n]

        @pl.when(page >= 0)
        def _():
            page_copy(n, page).start()

        @pl.when(page < 0)
        def _():
            empty_copy(n).start()

        return carry

    lax.fori_loop(0, slots, send, 0)
    grab.wait()
    width = span * rows
    held = window[...][:, :rows, :]
    keys = held[:, :, :HEAD_DIM].reshape(width, HEAD_DIM)
    values = held[:, :, HEAD_DIM:].reshape(width, HEAD_DIM)
    key_at = start * rows + lax.broadcasted_iota(jnp.int32, (rows, width), 1)
    query_at = block * rows + lax.broadcasted_iota(jnp.int32, (rows, width), 0)
    allowed = (key_at <= query_at) & (key_at >= first[...])
    for head in range(queries.shape[1] // HEAD_DIM):
        cols = pl.ds(head * HEAD_DIM, HEAD_DIM)
        scores = lax.dot_general(
            queries[:, cols], keys, (((1,), (1,)), ((), ())), preferred_element_type=f32
        ) * (HEAD_DIM**-0.5)
        scores = jnp.where(allowed, scores, masked_score)
        weights = jnp.where(allowed, jnp.exp(scores - jnp.max(scores, axis=1, keepdims=True)), 0.0)
        totals = jnp.sum(weights, axis=1, keepdims=True)
        mixed = jnp.dot(weights.astype(bf16), values, preferred_element_type=f32)
        attended[:, cols] = (mixed / totals).astype(bf16)
    load.wait()
    out_width = terms.shape[2]
    for half in range(2):
        cols = slice(2 * half * out_width, 2 * (half + 1) * out_width)
        part = jnp.dot(attended[...], wo[:, cols], preferred_element_type=f32).astype(bf16)
        terms[2 * half] = part[:, :out_width]
        terms[2 * half + 1] = part[:, out_width:]
    note.wait()
    ids = meta[:, :TOP, :HEAD_DIM].astype(f32)
    weight = meta[:, TOP : 2 * TOP, :HEAD_DIM].astype(f32) + meta[:, TOP : 2 * TOP, HEAD_DIM:].astype(f32)
    blocks = meta.shape[0]
    earlier = lax.broadcasted_iota(jnp.int32, (rows, rows), 0) < lax.broadcasted_iota(jnp.int32, (rows, rows), 1)
    earlier = earlier.astype(f32).astype(bf16)
    odd = lax.rem(lax.broadcasted_iota(jnp.int32, (blocks, rows), 0), PAIR).astype(f32) * CAP
    n_exp = slot.shape[0]
    for e in range(n_exp):
        hits = ids == (block * n_exp + e).astype(f32)
        named = jnp.max(hits.astype(f32), axis=1)
        rank = jnp.dot(named.astype(bf16), earlier, preferred_element_type=f32)
        place = jnp.where(named > 0.0, rank + odd, -1.0)
        slot[e] = jnp.concatenate([place.reshape(blocks // PAIR, PAIR, rows)[:, b] for b in range(PAIR)], axis=1)
        share = jnp.sum(jnp.where(hits, weight, 0.0), axis=1)
        gates[e] = jnp.concatenate([share.reshape(blocks // PAIR, PAIR, rows)[:, b] for b in range(PAIR)], axis=1)

    def settle(n, carry):
        empty_copy(n).wait()
        return carry

    lax.fori_loop(0, slots, settle, 0)


def attend(block, pages, queries, first, gathered, w_out, n_exp):
    blocks = gathered.shape[0]
    span = min(9, blocks)
    start = jnp.clip(block - 8, 0, blocks - span)
    width = gathered.shape[2]
    rows = queries.shape[0]
    terms = (RING, rows, w_out.shape[1] // RING)
    slot = (n_exp, blocks // PAIR, PAIR * rows)

    def whole(shape):
        return pl.BlockSpec(shape, lambda i, *_: (0,) * len(shape))

    return pl.pallas_call(
        attend_kernel,
        grid_spec=pltpu.PrefetchScalarGridSpec(
            num_scalar_prefetch=2,
            grid=(1,),
            in_specs=[whole(queries.shape), whole(first.shape), ANY, ANY],
            out_specs=(whole(terms), ANY, whole(slot), whole(slot)),
            scratch_shapes=[
                pltpu.VMEM((span,) + gathered.shape[1:], bf16),
                pltpu.VMEM((blocks, 16, width), bf16),
                pltpu.VMEM(w_out.shape, bf16),
                pltpu.VMEM((PAGE, width), bf16),
                pltpu.VMEM(queries.shape, bf16),
                pltpu.SemaphoreType.DMA((3,)),
                pltpu.SemaphoreType.DMA((pages.shape[0],)),
            ],
        ),
        out_shape=(
            jax.ShapeDtypeStruct(terms, bf16),
            jax.ShapeDtypeStruct((pages.shape[0], PAGE, width), bf16),
            jax.ShapeDtypeStruct(slot, f32),
            jax.ShapeDtypeStruct(slot, f32),
        ),
        compiler_params=pltpu.CompilerParams(vmem_limit_bytes=48 << 20),
        name="attend",
    )(jnp.stack([block, start]).astype(jnp.int32), pages, queries, first, gathered, w_out)


PAIR = 2


def expert_kernel(slot, gates, rows, w_gate, w_up, w_down, out, packed, scale, wgu, wd, sems):
    step = pl.program_id(0)
    groups = 8
    tokens = groups * UNIT[0]
    tiles = rows.shape[4] // groups
    quarter = tiles * UNIT[1]
    pair_cap = PAIR * CAP
    n_exp, _, ff = w_gate.shape
    loads = [
        pltpu.make_async_copy(src, dst, sems.at[n])
        for n, (src, dst) in enumerate(
            ((w_gate, wgu.at[:, :, pl.ds(0, ff)]), (w_up, wgu.at[:, :, pl.ds(ff, ff)]), (w_down, wd))
        )
    ]

    @pl.when(step == 0)
    def _():
        for load in loads:
            load.start()

    row = lax.broadcasted_iota(jnp.int32, (pair_cap, PAIR * tokens), 0).astype(f32)
    picks = []
    for z in range(RING):
        span = slice(z * pair_cap, (z + 1) * pair_cap)
        same = [
            jnp.broadcast_to(slot[e, pl.ds(step * RING + z, 1), :], row.shape) == row for e in range(n_exp)
        ]
        for e in range(n_exp):
            scale[e, span, :] = jnp.sum(
                jnp.where(same[e], gates[e, pl.ds(step * RING + z, 1), :], 0.0), axis=1, keepdims=True
            )
        picks.append(jnp.concatenate([m.astype(f32) for m in same], axis=0).astype(bf16))
        for h in range(2):
            parts = []
            for k in range(2):
                for j in range(tiles):
                    units = slice(j * groups, (j + 1) * groups)
                    parts.append(rows[0, z, :, 2 * h + k, units].reshape(PAIR * tokens, 128))
            got = jnp.dot(picks[z], jnp.concatenate(parts, axis=1), preferred_element_type=f32).astype(bf16)
            for e in range(n_exp):
                packed[e, span, 2 * h * quarter : 2 * (h + 1) * quarter] = got[e * pair_cap : (e + 1) * pair_cap]

    @pl.when(step == 0)
    def _():
        for load in loads:
            load.wait()

    for e in range(n_exp):
        both = jnp.dot(packed[e], wgu[e], preferred_element_type=f32)
        gate_term, up_term = both[:, :ff], both[:, ff:]
        act = (gate_term / (1.0 + jnp.exp(-gate_term)) * up_term).astype(bf16)
        for h in range(2):
            cols = slice(2 * h * quarter, 2 * (h + 1) * quarter)
            down = jnp.dot(act, wd[e, :, cols], preferred_element_type=f32)
            packed[e, :, cols] = (down * scale[e]).astype(bf16)
    for z in range(RING):
        span = slice(z * pair_cap, (z + 1) * pair_cap)
        for h in range(2):
            cols = slice(2 * h * quarter, 2 * (h + 1) * quarter)
            made = jnp.concatenate([packed[e, span, cols] for e in range(n_exp)], axis=0)
            back = lax.dot_general(picks[z], made, (((0,), (0,)), ((), ())), preferred_element_type=f32).astype(bf16)
            for k in range(2):
                for j in range(tiles):
                    n = k * tiles + j
                    out[0, z, :, 2 * h + k, j * groups : (j + 1) * groups] = back[:, n * 128 : (n + 1) * 128].reshape(
                        PAIR, groups, *UNIT
                    )


def experts(slot, gates, rows, w_gate, w_up, w_down):
    n_exp, width, ff = w_gate.shape
    taken = (n_exp, RING * PAIR * CAP)
    whole = pl.BlockSpec(slot.shape, lambda i: (0, 0, 0))
    some = pl.BlockSpec((1,) + rows.shape[1:], lambda i: (i,) + (0,) * (len(rows.shape) - 1))
    return pl.pallas_call(
        expert_kernel,
        grid=(RING,),
        in_specs=[whole, whole, some, ANY, ANY, ANY],
        out_specs=some,
        out_shape=jax.ShapeDtypeStruct(rows.shape, bf16),
        scratch_shapes=[
            pltpu.VMEM(taken + (width,), bf16),
            pltpu.VMEM(taken + (1,), f32),
            pltpu.VMEM((n_exp, width, 2 * ff), bf16),
            pltpu.VMEM(w_down.shape, bf16),
            pltpu.SemaphoreType.DMA((3,)),
        ],
        compiler_params=pltpu.CompilerParams(vmem_limit_bytes=56 << 20),
        name="experts",
    )(slot, gates, rows, w_gate, w_up, w_down)


def local(
    hidden, gain_attn, w_query, w_key, w_value, w_out, gain_moe, expert_ids, expert_gates,
    w_gate, w_up, w_down, seg_lengths, slot_page,
):
    tok_rows = hidden.shape[0]
    shard_count = lax.axis_size("seq")
    shard_index = lax.axis_index("seq")
    half_dim = HEAD_DIM // 2
    inverse = rope_base ** (-2.0 * jnp.arange(half_dim, dtype=f32) / HEAD_DIM)
    inverse = jnp.concatenate([inverse, inverse])[None, :]
    gate_high = lax.reduce_precision(expert_gates, 8, 7)
    gate_low = expert_gates - gate_high
    blank = jnp.zeros((tok_rows, 2 * HEAD_DIM), f32)
    routing = jnp.concatenate(
        [expert_ids.astype(f32), gate_high, blank[:, : 16 - TOP], gate_low, blank[:, : HEAD_DIM - 16 - 2 * TOP]], axis=1
    )
    gathered, queries, first = front(
        seg_lengths, hidden, gain_attn[None, :], inverse, routing, w_query, w_key, w_value
    )
    gathered = gathered.reshape((shard_count,) + gathered.shape[3:])
    slot_count = slot_page.shape[0] // shard_count
    own_slots = lax.dynamic_slice_in_dim(slot_page, shard_index * slot_count, slot_count)
    terms, kv_cache, slot, gates = attend(
        shard_index, own_slots, queries, first, gathered, w_out, w_gate.shape[0]
    )
    rows, mid = row_gather(terms, hidden, gain_moe[None, :])
    made = experts(slot, gates, rows, w_gate, w_up, w_down)
    return (row_sum(made, mid), kv_cache)


def solution(mesh):
    placed = (
        P("seq", None),
        P(),
        P(None, "tp"),
        P(None, "tp"),
        P(None, "tp"),
        P("tp", None),
        P(),
        P("seq", None),
        P("seq", None),
        P("seq", None, "tp"),
        P("seq", None, "tp"),
        P("seq", "tp", None),
        P(),
        P(),
    )
    return jax.shard_map(
        local,
        mesh=mesh,
        in_specs=placed,
        out_specs=(P("seq", "tp"), P("seq", None, "tp")),
        check_vma=False,
    )
```

time: 239 us -> 195 us (0.82)
  Pallas kernels: 204 us -> 184 us
  matrix products: 11.8 us -> 0 us
  local copies, waits for them, and re-layouts: 14.9 us -> 7.95 us
  other arithmetic: 6.81 us -> 1.56 us
    pallas_call x1, Pallas kernels: 66.8 us -> 53.5 us  [row_sum(): pl.pallas_call(kernel, out_shape=jax.ShapeDtypeStruct((rows, cols), bf16)...]
    dot_general x8 -> x0, matrix products: 11.8 us -> none  [the longest x4 5.87 us: local(): jnp.dot(attended, w_out[:, q * quarter:(q + 1) * quarter], preferred_elem...]
    pallas_call x1, Pallas kernels: 76.3 us -> 65.5 us  [row_gather(): pl.pallas_call(row_gather_kernel, out_shape=(jax.ShapeDtypeStruct((RING,...]
    unnamed x15 -> x16, local copies, waits for them, and re-layouts: 9.33 us -> 5.39 us
    pallas_call x2, Pallas kernels: 55.6 us -> 59 us  [the longest x1 34.1 us: experts(): pl.pallas_call(expert_kernel, grid=(RING,), in_specs=[whole, whole, some,...]
    reshape x5 -> x0, local copies, waits for them, and re-layouts: 2.6 us -> none  [the longest x4 2.59 us: paired(): values.reshape(shard_count // PAIR, PAIR, n_exp, tok_rows).swapaxes(1, 2)]
where the time goes in v2:
time: 195 us; the launch traced here: 194 us
  Pallas kernels  184 us (94%)
  local copies, waits for them, and re-layouts  7.95 us (4%)
    pallas_call x1, Pallas kernels, row_gather(): pl.pallas_call(row_gather_kernel, out_shape=(jax.ShapeDtypeStruct((RING,...  65.5 us
    pallas_call x1, Pallas kernels, row_sum(): pl.pallas_call(kernel, out_shape=jax.ShapeDtypeStruct((rows, cols), bf16)...  53.5 us
    pallas_call x1, Pallas kernels, experts(): pl.pallas_call(expert_kernel, grid=(RING,), in_specs=[whole, whole, some,...  34.1 us
    pallas_call x1, Pallas kernels, front(): pl.pallas_call(front_kernel, out_shape=(jax.ShapeDtypeStruct((RING, RING,...  24.9 us
    pallas_call x1, Pallas kernels, attend(): pl.pallas_call(attend_kernel, grid_spec=pltpu.PrefetchScalarGridSpec(num_...  6.08 us
    unnamed x16, local copies, waits for them, and re-layouts  5.39 us

profile of v2, /device:TPU:0, one launch (start us, length us, event | category | flops | bytes accessed | tf_op | source)
XLA Modules:
  0.0 194.3 jit_solution(8881417670715086900)
XLA Ops:
  0.6 0.1 pad_add_fusion.where
  0.7 0.8 dynamic_slice.3.pages
  1.5 0.1 maximum_bitcast_fusion.inverse
  1.6 0.7 convert_element_type.3
  2.3 0.7 reduce_precision.3
  2.9 0.7 broadcast_in_dim.9.gain
  3.7 0.7 broadcast_in_dim.11.gain
  4.4 0.1 copy.22
  4.5 0.1 copy.21
  4.6 0.8 copy.19
  5.4 0.1 concatenate.7.routing
  5.6 0.0 copy-start
  5.6 1.1 copy-done
  6.7 1.1 copy-done.2
  7.8 1.1 copy-done.3
  8.8 0.7 copy-done.6
  9.5 24.9 %front.1 = (bf16[4,4,2,144,256]{4,3,2,1,0:T(8,128)(2,1)S(1)}, bf16[128,640]{1,0:T(8,128)(2,1)S(1)}, s32[128,1]{1,0:T(8,128)S(1)}) custom-call(s32[16]{0:T(128)S(1)} %copy-done.6, bf16[128,2560]{1,0:T(8,128)(2,1)S(1)} %copy-done, f32[1,2560]{1,0:T(1,128)S(1)} %broadcast_in_dim.9.gain, f32[1,128]{1,0:T(1,128)S(1)} %maximum_bitcast_fusion.inverse, ...), custom_call_target="tpu_custom_call" | custom-call | tf_op jit(solution)/shard_map/front/pallas_call | solution.py:288
  34.4 0.0 copy-start.1
  34.4 6.1 %attend.1 = (bf16[4,128,640]{2,1,0:T(8,128)(2,1)S(1)}, bf16[64,16,256]{2,1,0:T(8,128)(2,1)}, f32[2,16,256]{2,1,0:T(8,128)S(1)}, f32[2,16,256]{2,1,0:T(8,128)S(1)}) custom-call(s32[2]{0:T(128)S(1)} %pad_add_fusion.where, s32[64]{0:T(128)S(1)} %dynamic_slice.3.pages, bf16[128,640]{1,0:T(8,128)(2,1)S(1)} %get-tuple-element.11.queries, ...), custom_call_target="tpu_custom_call" | custom-call | tf_op jit(solution)/shard_map/attend/pallas_call | solution.py:626
  40.5 0.0 copy-start.4
  40.5 65.5 %row_gather.1 = (bf16[4,4,2,4,40,16,128]{6,5,4,3,2,1,0:T(8,128)(2,1)}, bf16[128,640]{1,0:T(8,128)(2,1)S(1)}) custom-call(bf16[4,128,640]{2,1,0:T(8,128)(2,1)S(1)} %get-tuple-element.16.terms, bf16[128,2560]{1,0:T(8,128)(2,1)S(1)} %copy-done.1, f32[1,2560]{1,0:T(1,128)S(1)} %broadcast_in_dim.11.gain), custom_call_target="tpu_custom_call" | custom-call | tf_op jit(solution)/shard_map/row_gather/pallas_call | solution.py:356
  106.0 34.1 %experts.1.terms = bf16[4,4,2,4,40,16,128]{6,5,4,3,2,1,0:T(8,128)(2,1)} custom-call(f32[2,16,256]{2,1,0:T(8,128)} %copy-done.4, f32[2,16,256]{2,1,0:T(8,128)} %copy-done.5, bf16[4,4,2,4,40,16,128]{6,5,4,3,2,1,0:T(8,128)(2,1)} %get-tuple-element.17.rows, bf16[2,2560,384]{2,1,0:T(8,128)(2,1)} %w_gate.1, bf16[2,2560,384]{2,1,0:T(8,128)(2,1)} %w_up.1, ...), custom_call_target="tpu_custom_call" | custom-call | tf_op jit(solution)/shard_map/experts/pallas_call | solution.py:731
  140.2 53.5 %row_sum.1 = bf16[128,640]{1,0:T(8,128)(2,1)S(1)} custom-call(bf16[4,4,2,4,40,16,128]{6,5,4,3,2,1,0:T(8,128)(2,1)} %experts.1.terms, bf16[128,640]{1,0:T(8,128)(2,1)S(1)} %get-tuple-element.18.mid), custom_call_target="tpu_custom_call" | custom-call | tf_op jit(solution)/shard_map/row_sum/pallas_call | solution.py:502
  193.7 0.7 copy.24
  (11 shorter events, 0.0 us)
Async XLA Ops:
  5.6 1.1 copy-start
  6.7 1.1 copy-start.2
  7.8 1.1 copy-start.3
  8.8 0.7 copy-start.6
  34.4 6.1 %copy-start.1 = (bf16[128,2560]{1,0:T(8,128)(2,1)S(1)}, bf16[128,2560]{1,0:T(8,128)(2,1)}, u32[]{:S(2)}) copy-start(bf16[128,2560]{1,0:T(8,128)(2,1)} %hidden.3) | copy-start | bytes 1966084
  40.5 65.5 %copy-start.4 = (f32[2,16,256]{2,1,0:T(8,128)}, f32[2,16,256]{2,1,0:T(8,128)S(1)}, u32[]{:S(2)}) copy-start(f32[2,16,256]{2,1,0:T(8,128)S(1)} %get-tuple-element.14.slot) | copy-start | bytes 98308
  40.5 65.5 %copy-start.5 = (f32[2,16,256]{2,1,0:T(8,128)}, f32[2,16,256]{2,1,0:T(8,128)S(1)}, u32[]{:S(2)}) copy-start(f32[2,16,256]{2,1,0:T(8,128)S(1)} %get-tuple-element.15.gates) | copy-start | bytes 98308

commit v3 on v2

--- a/solution.py
+++ b/solution.py
@@ -2,6 +2,7 @@
 
 import jax
 import jax.numpy as jnp
+import numpy as np
 from jax import lax
 from jax.experimental import pallas as pl
 from jax.experimental.pallas import tpu as pltpu
@@ -74,7 +75,7 @@
             copy.wait_send()
 
 
-def torus_gather(me, dims, parts, src, out, links, local_sem, beside=None):
+def torus_gather(me, dims, parts, src, out, links, local_sem, beside):
     sibling = moved(me, "c", 1)
 
     def at(where, row0, rows):
@@ -83,56 +84,36 @@
     own = {d: me[d] for d in dims}
     local = pltpu.make_async_copy(src, at(own, 0, src.shape[0]), local_sem)
     local.start()
-    to_sibling = [links.push(src, at(own, 0, src.shape[0]), sibling)]
-    for phase in range(len(parts[0][3])):
+    to_sibling = []
+    for phase in range(len(parts[0][2])):
         if phase == 1:
             local.wait()
         live = []
-        for row0, rows, half, order in parts:
+        for row0, rows, order in parts:
             axis = order[phase]
             base = dict(own)
             for done in order[:phase]:
                 base[done] = slice(None)
             whole = at(base, row0, rows)
             source = src.at[pl.ds(row0, rows), :] if phase == 0 else whole
-            up = links.push(source, whole, moved(me, axis, 1))
-            down = links.push(source, whole, moved(me, axis, -1))
-            live.append((row0, rows, half, order, axis, base, up, down))
-        if phase == 0 and beside is not None:
+            for step in (1, -1, 2):
+                live.append((row0, rows, axis, base, step, links.push(source, whole, moved(me, axis, step))))
+        if phase == 0:
+            to_sibling.append(links.push(src, at(own, 0, src.shape[0]), sibling))
             beside()
-        forwarded = []
-        for row0, rows, half, order, axis, base, up, down in live:
-            for copy, step in ((up, 1), (down, -1)):
-                copy.wait_recv()
-                got = dict(base)
-                got[axis] = moved(me, axis, -step)[axis]
-                if phase == 0:
-                    r0, rn = (row0, half) if step == 1 else (row0 + half, rows - half)
-                    piece = at(got, r0, rn)
-                else:
-                    cut = dict(got)
-                    cut[order[0]] = pl.ds(0, 2) if step == 1 else pl.ds(2, 2)
-                    piece = at(cut, row0, rows)
-                forwarded.append(links.push(piece, piece, moved(me, axis, step)))
-                there = at(got, row0, rows)
-                to_sibling.append(links.push(there, there, sibling))
-        for n, (row0, rows, half, order, axis, base, up, down) in enumerate(live):
-            forwarded[2 * n].wait_recv()
-            forwarded[2 * n + 1].wait_recv()
-            got = dict(base)
-            got[axis] = moved(me, axis, 2)[axis]
-            there = at(got, row0, rows)
+        for row0, rows, axis, base, step, copy in live:
+            copy.wait_recv()
+            there = at({**base, axis: moved(me, axis, -step)[axis]}, row0, rows)
             to_sibling.append(links.push(there, there, sibling))
     for copy in to_sibling:
         copy.wait_recv()
 
 
 def copies_of_gather(parts):
-    phases = len(parts[0][3])
-    return 1 + phases * len(parts) * 7
-
-
-KV_PARTS = ((0, 80, 48, ("x", "z")), (80, 64, 32, ("z", "x")))
+    return 1 + len(parts[0][2]) * len(parts) * 6
+
+
+KV_PARTS = ((0, 80, ("x", "z")), (80, 64, ("z", "x")))
 UNIT = (16, 128)
 ROW_PARTS = (
     (0, 14, ("z", "y", "x")),
@@ -232,8 +213,12 @@
     return one * cosine + pltpu.roll(one, HEAD_DIM // 2, 1) * sine
 
 
+def flat_gain(gain, first, count):
+    return jnp.concatenate([gain[pl.ds(first + j, 1), :] for j in range(count)], axis=1)
+
+
 def front_kernel(
-    lengths, hidden, gain, inverse, routing, w_query, w_key, w_value,
+    lengths, hidden, gain, inverse, expert_ids, expert_gates, w_query, w_key, w_value,
     gathered, queries, first, sent, wq, wk, wv, normed, send_sem, recv_sem, local_sem,
 ):
     me = my_place()
@@ -258,16 +243,26 @@
     sine = jnp.where(lane < HEAD_DIM // 2, -jnp.sin(angles), jnp.sin(angles))
     wide = hidden[...].astype(f32)
     factor = lax.rsqrt(jnp.mean(wide * wide, axis=1, keepdims=True) + epsilon)
-    normed[...] = (wide * factor * gain[...]).astype(bf16)
-    turned = routing[...].T
-    sent[rows : rows + 16, :HEAD_DIM] = turned[:16].astype(bf16)
-    sent[rows : rows + 16, HEAD_DIM:] = turned[16:32].astype(bf16)
+    normed[...] = (wide * factor * flat_gain(gain, 0, gain.shape[0])).astype(bf16)
+    high = expert_gates[...].astype(bf16)
+    low = (expert_gates[...] - high.astype(f32)).astype(bf16)
+    to_at = lax.broadcasted_iota(jnp.int32, (16, TOP), 0)
+    from_at = lax.broadcasted_iota(jnp.int32, (16, TOP), 1)
+    top = (from_at == to_at).astype(f32).astype(bf16)
+    below = (from_at + 8 == to_at).astype(f32).astype(bf16)
+
+    def placed(where, values):
+        return jnp.dot(where, values, preferred_element_type=f32)
+
+    listed = placed(top, expert_ids[...].astype(f32).astype(bf16)) + placed(below, high)
+    sent[rows : rows + 16, :HEAD_DIM] = listed.astype(bf16)
+    sent[rows : rows + 16, HEAD_DIM:] = placed(below, low).astype(bf16)
     loads[0].wait()
     key = jnp.dot(normed[...], wk[...], preferred_element_type=f32)
     sent[:rows, :HEAD_DIM] = turn(key, cosine, sine).astype(bf16)
     loads[1].wait()
     sent[:rows, HEAD_DIM:] = jnp.dot(normed[...], wv[...], preferred_element_type=f32).astype(bf16)
-    enter([moved(me, a, s) for a in ("x", "z") for s in (1, -1)] + [moved(me, "c", 1)])
+    enter([moved(me, a, s) for a in ("x", "z") for s in (1, -1, 2)] + [moved(me, "c", 1)])
     links = Links(send_sem, recv_sem)
 
     def beside():
@@ -281,7 +276,7 @@
     links.finish()
 
 
-def front(lengths, hidden, gain, inverse, routing, w_query, w_key, w_value):
+def front(lengths, hidden, gain, inverse, expert_ids, expert_gates, w_query, w_key, w_value):
     n = copies_of_gather(KV_PARTS)
     rows = hidden.shape[0]
     width = w_key.shape[1] + w_value.shape[1]
@@ -292,7 +287,7 @@
             jax.ShapeDtypeStruct((rows, w_query.shape[1]), bf16),
             jax.ShapeDtypeStruct((rows, 1), jnp.int32),
         ),
-        in_specs=[pl.BlockSpec(memory_space=pltpu.SMEM)] + [WHOLE] * 4 + [ANY] * 3,
+        in_specs=[pl.BlockSpec(memory_space=pltpu.SMEM)] + [WHOLE] * 5 + [ANY] * 3,
         out_specs=(ANY, WHOLE, WHOLE),
         scratch_shapes=[
             pltpu.VMEM((rows + 16, width), bf16),
@@ -305,10 +300,10 @@
             pltpu.SemaphoreType.DMA((4,)),
         ],
         compiler_params=pltpu.CompilerParams(
-            collective_id=1, has_side_effects=True, vmem_limit_bytes=48 << 20
+            collective_id=1, has_side_effects=True, vmem_limit_bytes=58 << 20
         ),
         name="front",
-    )(lengths, hidden, gain, inverse, routing, w_query, w_key, w_value)
+    )(lengths, hidden, gain, inverse, expert_ids, expert_gates, w_query, w_key, w_value)
 
 
 def row_gather_kernel(
@@ -339,7 +334,7 @@
         whole = whole + squares[n]
     whole = jnp.broadcast_to(whole[:1], (128, 128)).T[:, :1]
     factor = lax.rsqrt(whole * (1.0 / (RING * wide.shape[1])) + epsilon)
-    ready = (wide * factor * gain[:, mine]).astype(bf16)
+    ready = (wide * factor * flat_gain(gain, me["y"] * (width // 128), width // 128)).astype(bf16)
     for j, tile in enumerate(to_units(ready)):
         row_v[j * tile.shape[0] : (j + 1) * tile.shape[0]] = tile
     keep = pltpu.make_async_copy(mid_v, mid, local_sem.at[1])
@@ -524,23 +519,21 @@
 
 def attend_kernel(
     where, pages, queries, first, gathered, w_out, terms, cache, slot, gates,
-    window, meta, wo, zeros, attended, sems, page_sems,
+    full, wo, zeros, attended, sems, page_sems,
 ):
-    span = window.shape[0]
+    span = min(9, full.shape[0])
     block, start = where[0], where[1]
     slots = cache.shape[0]
     rows = queries.shape[0]
-    grab = pltpu.make_async_copy(gathered.at[pl.ds(start, span)], window, sems.at[0])
+    grab = pltpu.make_async_copy(gathered, full, sems.at[0])
     grab.start()
-    note = pltpu.make_async_copy(gathered.at[:, pl.ds(rows, 16), :], meta, sems.at[1])
-    note.start()
-    load = pltpu.make_async_copy(w_out, wo, sems.at[2])
+    load = pltpu.make_async_copy(w_out, wo, sems.at[1])
     load.start()
     zeros[...] = jnp.zeros_like(zeros)
 
     def page_copy(n, page):
         return pltpu.make_async_copy(
-            gathered.at[page // 8, pl.ds(pl.multiple_of(lax.rem(page, 8) * PAGE, PAGE), PAGE), :],
+            full.at[page // 8, pl.ds(pl.multiple_of(lax.rem(page, 8) * PAGE, PAGE), PAGE), :],
             cache.at[n],
             page_sems.at[n],
         )
@@ -561,10 +554,10 @@
 
         return carry
 
+    grab.wait()
     lax.fori_loop(0, slots, send, 0)
-    grab.wait()
     width = span * rows
-    held = window[...][:, :rows, :]
+    held = full[pl.ds(start, span), :rows, :]
     keys = held[:, :, :HEAD_DIM].reshape(width, HEAD_DIM)
     values = held[:, :, HEAD_DIM:].reshape(width, HEAD_DIM)
     key_at = start * rows + lax.broadcasted_iota(jnp.int32, (rows, width), 1)
@@ -587,9 +580,9 @@
         part = jnp.dot(attended[...], wo[:, cols], preferred_element_type=f32).astype(bf16)
         terms[2 * half] = part[:, :out_width]
         terms[2 * half + 1] = part[:, out_width:]
-    note.wait()
+    meta = full[:, rows : rows + 16, :]
     ids = meta[:, :TOP, :HEAD_DIM].astype(f32)
-    weight = meta[:, TOP : 2 * TOP, :HEAD_DIM].astype(f32) + meta[:, TOP : 2 * TOP, HEAD_DIM:].astype(f32)
+    weight = meta[:, 8 : 8 + TOP, :HEAD_DIM].astype(f32) + meta[:, 8 : 8 + TOP, HEAD_DIM:].astype(f32)
     blocks = meta.shape[0]
     earlier = lax.broadcasted_iota(jnp.int32, (rows, rows), 0) < lax.broadcasted_iota(jnp.int32, (rows, rows), 1)
     earlier = earlier.astype(f32).astype(bf16)
@@ -611,7 +604,7 @@
     lax.fori_loop(0, slots, settle, 0)
 
 
-def attend(block, pages, queries, first, gathered, w_out, n_exp):
+def attend(block, pages, slots, queries, first, gathered, w_out, n_exp):
     blocks = gathered.shape[0]
     span = min(9, blocks)
     start = jnp.clip(block - 8, 0, blocks - span)
@@ -631,22 +624,21 @@
             in_specs=[whole(queries.shape), whole(first.shape), ANY, ANY],
             out_specs=(whole(terms), ANY, whole(slot), whole(slot)),
             scratch_shapes=[
-                pltpu.VMEM((span,) + gathered.shape[1:], bf16),
-                pltpu.VMEM((blocks, 16, width), bf16),
+                pltpu.VMEM(gathered.shape, bf16),
                 pltpu.VMEM(w_out.shape, bf16),
                 pltpu.VMEM((PAGE, width), bf16),
                 pltpu.VMEM(queries.shape, bf16),
-                pltpu.SemaphoreType.DMA((3,)),
-                pltpu.SemaphoreType.DMA((pages.shape[0],)),
+                pltpu.SemaphoreType.DMA((2,)),
+                pltpu.SemaphoreType.DMA((slots,)),
             ],
         ),
         out_shape=(
             jax.ShapeDtypeStruct(terms, bf16),
-            jax.ShapeDtypeStruct((pages.shape[0], PAGE, width), bf16),
+            jax.ShapeDtypeStruct((slots, PAGE, width), bf16),
             jax.ShapeDtypeStruct(slot, f32),
             jax.ShapeDtypeStruct(slot, f32),
         ),
-        compiler_params=pltpu.CompilerParams(vmem_limit_bytes=48 << 20),
+        compiler_params=pltpu.CompilerParams(vmem_limit_bytes=58 << 20),
         name="attend",
     )(jnp.stack([block, start]).astype(jnp.int32), pages, queries, first, gathered, w_out)
 
@@ -750,28 +742,20 @@
     hidden, gain_attn, w_query, w_key, w_value, w_out, gain_moe, expert_ids, expert_gates,
     w_gate, w_up, w_down, seg_lengths, slot_page,
 ):
-    tok_rows = hidden.shape[0]
     shard_count = lax.axis_size("seq")
     shard_index = lax.axis_index("seq")
-    half_dim = HEAD_DIM // 2
-    inverse = rope_base ** (-2.0 * jnp.arange(half_dim, dtype=f32) / HEAD_DIM)
-    inverse = jnp.concatenate([inverse, inverse])[None, :]
-    gate_high = lax.reduce_precision(expert_gates, 8, 7)
-    gate_low = expert_gates - gate_high
-    blank = jnp.zeros((tok_rows, 2 * HEAD_DIM), f32)
-    routing = jnp.concatenate(
-        [expert_ids.astype(f32), gate_high, blank[:, : 16 - TOP], gate_low, blank[:, : HEAD_DIM - 16 - 2 * TOP]], axis=1
-    )
+    steps = np.arange(HEAD_DIM, dtype=np.float32) % (HEAD_DIM // 2)
+    inverse = jnp.asarray(np.float32(rope_base) ** (np.float32(-2.0) * steps / np.float32(HEAD_DIM)))[None, :]
     gathered, queries, first = front(
-        seg_lengths, hidden, gain_attn[None, :], inverse, routing, w_query, w_key, w_value
+        seg_lengths, hidden, gain_attn.reshape(-1, 128), inverse, expert_ids.T, expert_gates.T, w_query, w_key, w_value
     )
     gathered = gathered.reshape((shard_count,) + gathered.shape[3:])
     slot_count = slot_page.shape[0] // shard_count
     own_slots = lax.dynamic_slice_in_dim(slot_page, shard_index * slot_count, slot_count)
     terms, kv_cache, slot, gates = attend(
-        shard_index, own_slots, queries, first, gathered, w_out, w_gate.shape[0]
+        shard_index, own_slots, slot_count, queries, first, gathered, w_out, w_gate.shape[0]
     )
-    rows, mid = row_gather(terms, hidden, gain_moe[None, :])
+    rows, mid = row_gather(terms, hidden, gain_moe.reshape(-1, 128))
     made = experts(slot, gates, rows, w_gate, w_up, w_down)
     return (row_sum(made, mid), kv_cache)
 

time: 195 us -> 191 us (0.979)
  local copies, waits for them, and re-layouts: 7.95 us -> 3.06 us
  Pallas kernels: 184 us -> 186 us
    unnamed x16 -> x7, local copies, waits for them, and re-layouts: 5.39 us -> 1.76 us
    pallas_call x1, Pallas kernels: 6.08 us -> 9.07 us  [attend(): pl.pallas_call(attend_kernel, grid_spec=pltpu.PrefetchScalarGridSpec(num_...]
where the time goes in v3:
time: 191 us
  Pallas kernels  186 us (97%)
  local copies, waits for them, and re-layouts  3.06 us (2%)
    pallas_call x1, Pallas kernels, row_gather(): pl.pallas_call(row_gather_kernel, out_shape=(jax.ShapeDtypeStruct((RING,...  64.7 us
    pallas_call x1, Pallas kernels, row_sum(): pl.pallas_call(kernel, out_shape=jax.ShapeDtypeStruct((rows, cols), bf16)...  54.5 us
    pallas_call x1, Pallas kernels, experts(): pl.pallas_call(expert_kernel, grid=(RING,), in_specs=[whole, whole, some,...  34 us
    pallas_call x1, Pallas kernels, front(): pl.pallas_call(front_kernel, out_shape=(jax.ShapeDtypeStruct((RING, RING,...  24.3 us
    pallas_call x1, Pallas kernels, attend(): pl.pallas_call(attend_kernel, grid_spec=pltpu.PrefetchScalarGridSpec(num_...  9.07 us

profile of v3, /device:TPU:0, one launch (start us, length us, event | category | flops | bytes accessed | tf_op | source)
XLA Modules:
  0.0 190.9 jit_solution(3164638086065056637)
XLA Ops:
  0.6 0.6 pad_add_fusion.where
  1.3 1.3 dynamic_slice.3.pages
  2.6 24.3 %front.1 = (bf16[4,4,2,144,256]{4,3,2,1,0:T(8,128)(2,1)}, bf16[128,640]{1,0:T(8,128)(2,1)}, s32[128,1]{1,0:T(8,128)}) custom-call(s32[16]{0:T(128)} %lengths.1, bf16[128,2560]{1,0:T(8,128)(2,1)} %hidden.3, f32[20,128]{1,0:T(8,128)} %bitcast.9, f32[1,128]{1,0:T(1,128)} %constant.23.inverse, s32[6,128]{1,0:T(8,128)} %bitcast.10, f32[6,128]{1,0:T(8,128)} %bitcast.11, ...), custom_call_target="tpu_custom_call" | custom-call | tf_op jit(solution)/shard_map/front/pallas_call | solution.py:283
  26.9 0.0 copy-start
  26.9 0.0 copy-start.2
  26.9 9.1 %attend.1 = (bf16[4,128,640]{2,1,0:T(8,128)(2,1)}, bf16[64,16,256]{2,1,0:T(8,128)(2,1)}, f32[2,16,256]{2,1,0:T(8,128)}, f32[2,16,256]{2,1,0:T(8,128)}) custom-call(s32[2]{0:T(128)} %pad_add_fusion.where, s32[64]{0:T(128)} %dynamic_slice.3.pages, bf16[128,640]{1,0:T(8,128)(2,1)} %get-tuple-element.11.queries, s32[128,1]{1,0:T(8,128)} %get-tuple-element.12.first, ...), custom_call_target="tpu_custom_call" | custom-call | tf_op jit(solution)/shard_map/attend/pallas_call | solution.py:619
  36.0 0.0 copy-done
  36.0 0.0 copy-done.2
  36.0 0.0 copy-start.1
  36.0 1.1 copy-done.1
  37.1 64.7 %row_gather.1 = (bf16[4,4,2,4,40,16,128]{6,5,4,3,2,1,0:T(8,128)(2,1)}, bf16[128,640]{1,0:T(8,128)(2,1)S(1)}) custom-call(bf16[4,128,640]{2,1,0:T(8,128)(2,1)S(1)} %copy-done.1, bf16[128,2560]{1,0:T(8,128)(2,1)S(1)} %copy-done, f32[20,128]{1,0:T(8,128)S(1)} %bitcast.7), custom_call_target="tpu_custom_call" | custom-call | tf_op jit(solution)/shard_map/row_gather/pallas_call | solution.py:351
  101.8 34.0 %experts.1.terms = bf16[4,4,2,4,40,16,128]{6,5,4,3,2,1,0:T(8,128)(2,1)} custom-call(f32[2,16,256]{2,1,0:T(8,128)} %get-tuple-element.14.slot, f32[2,16,256]{2,1,0:T(8,128)} %get-tuple-element.15.gates, bf16[4,4,2,4,40,16,128]{6,5,4,3,2,1,0:T(8,128)(2,1)} %get-tuple-element.17.rows, bf16[2,2560,384]{2,1,0:T(8,128)(2,1)} %w_gate.1, ...), custom_call_target="tpu_custom_call" | custom-call | tf_op jit(solution)/shard_map/experts/pallas_call | solution.py:723
  135.7 54.5 %row_sum.1 = bf16[128,640]{1,0:T(8,128)(2,1)S(1)} custom-call(bf16[4,4,2,4,40,16,128]{6,5,4,3,2,1,0:T(8,128)(2,1)} %experts.1.terms, bf16[128,640]{1,0:T(8,128)(2,1)S(1)} %get-tuple-element.18.mid), custom_call_target="tpu_custom_call" | custom-call | tf_op jit(solution)/shard_map/row_sum/pallas_call | solution.py:497
  190.2 0.7 copy.18
Async XLA Ops:
  26.9 9.1 %copy-start = (bf16[128,2560]{1,0:T(8,128)(2,1)S(1)}, bf16[128,2560]{1,0:T(8,128)(2,1)}, u32[]{:S(2)}) copy-start(bf16[128,2560]{1,0:T(8,128)(2,1)} %hidden.3) | copy-start | bytes 1966084
  26.9 9.1 %copy-start.2 = (f32[2560]{0:T(1024)S(1)}, f32[2560]{0:T(1024)}, u32[]{:S(2)}) copy-start(f32[2560]{0:T(1024)} %param.21) | copy-start | bytes 30724
  36.0 1.1 copy-start.1

commit v4 on v3

--- a/solution.py
+++ b/solution.py
@@ -376,14 +376,50 @@
 SUM_STREAMS = ((2, 1), (1, -1), (-1, 1), (0, -1))
 
 
-def row_sum_kernel(terms, mid, out, total, other, bufs, out_v, send_sem, recv_sem, local_sem):
+def row_sum_kernel(slot, source, mid, out, terms, made, other, bufs, out_v, send_sem, recv_sem, local_sem, in_sems):
     me = my_place()
+    takes = []
+    for x in range(RING):
+        rows = pl.ds(x * RING * PAIR * CAP, RING * PAIR * CAP)
+        takes.append(pltpu.make_async_copy(source.at[:, rows, :], made.at[:, rows, :], in_sems.at[x]))
+        takes[x].start()
     sibling = moved(me, "c", 1)
     enter([moved(me, a, s) for a in ("x", "z", "y") for s in (1, -1, 2)] + [sibling])
     links = Links(send_sem, recv_sem)
 
-    def held(ref, where, u0, n):
-        return ref.at[tuple(where[d] for d in SUM_DIMS) + (pl.ds(u0, n),)]
+    groups = 8
+    tokens = groups * UNIT[0]
+    tiles = terms.shape[4] // groups
+    pair_cap = PAIR * CAP
+    n_exp, _, width = made.shape
+
+    def spread(x, z):
+        chip = x * RING + z
+        at = pl.multiple_of(chip * pair_cap, 16)
+        row = lax.broadcasted_iota(jnp.int32, (pair_cap, PAIR * tokens), 0).astype(f32)
+        same = [jnp.broadcast_to(slot[e, pl.ds(chip, 1), :], row.shape) == row for e in range(n_exp)]
+        pick = jnp.concatenate([m.astype(f32) for m in same], axis=0).astype(bf16)
+        for h in range(2):
+            cols = slice(h * width // 2, (h + 1) * width // 2)
+            rows = jnp.concatenate([made[e, pl.ds(at, pair_cap), cols] for e in range(n_exp)], axis=0)
+            back = lax.dot_general(pick, rows, (((0,), (0,)), ((), ())), preferred_element_type=f32).astype(bf16)
+            for k in range(2):
+                for j in range(tiles):
+                    n = k * tiles + j
+                    terms[x, z, :, 2 * h + k, j * groups : (j + 1) * groups] = back[:, n * 128 : (n + 1) * 128].reshape(
+                        PAIR, groups, *UNIT
+                    )
+
+    def one_chip(chip, carry):
+        spread(chip // RING, lax.rem(chip, RING))
+        return carry
+
+    for x in range(RING):
+        takes[x].wait()
+        lax.fori_loop(x * RING, (x + 1) * RING, one_chip, 0)
+
+    def held(where, u0, n):
+        return terms.at[where["x"], where["z"], me["c"], where["y"], pl.ds(u0, n)]
 
     def place(p, stream, **free):
         order = ROW_PARTS[p][2]
@@ -396,30 +432,23 @@
     for stream in range(4):
         for p, (u0, n, order) in enumerate(ROW_PARTS):
             where = place(p, stream, **{order[1]: slice(None), order[2]: slice(None)})
-            slot = stream * 3 + p
-            keep = pltpu.make_async_copy(
-                terms.at[where["x"], where["z"], me["c"], where["y"], pl.ds(u0, n)],
-                held(total, where, u0, n),
-                local_sem.at[slot],
-            )
-            keep.start()
-            push = links.push(
+            first[p, stream] = links.push(
                 terms.at[where["x"], where["z"], sibling["c"], where["y"], pl.ds(u0, n)],
-                held(other, where, u0, n),
+                other.at[where["x"], where["z"], where["y"], pl.ds(u0, n)],
                 sibling,
             )
-            first[p, stream] = (keep, push)
 
     def add(where, u0, n, buf, lead):
         span = pl.ds(u0, n)
         if lead is None:
-            index = tuple(where[d] for d in SUM_DIMS) + (span,)
-            total[index] = total[index] + buf[...]
+            index = (where["x"], where["z"], me["c"], where["y"], span)
+            terms[index] = terms[index] + buf[...]
             return
 
         def one(k, carry):
-            index = tuple(k if d == lead else where[d] for d in SUM_DIMS) + (span,)
-            total[index] = total[index] + buf[k]
+            spot = {**where, lead: k}
+            index = (spot["x"], spot["z"], me["c"], spot["y"], span)
+            terms[index] = terms[index] + buf[k]
             return carry
 
         lax.fori_loop(0, RING, one, 0)
@@ -429,16 +458,14 @@
         step, way = SUM_STREAMS[stream]
         for p, (u0, n, order) in enumerate(ROW_PARTS):
             if stage == 0:
-                keep, push = first[p, stream]
-                keep.wait()
-                push.wait_recv()
+                first[p, stream].wait_recv()
                 where = place(p, stream)
                 span = pl.ds(u0, n)
 
                 def one(k, carry, where=where, span=span, order=order):
                     spot = {order[1]: k // RING, order[2]: lax.rem(k, RING)}
-                    index = tuple(spot.get(d, where[d]) for d in SUM_DIMS) + (span,)
-                    total[index] = total[index] + other[index]
+                    x, z, y = (spot.get(d, where[d]) for d in SUM_DIMS)
+                    terms[x, z, me["c"], y, span] = terms[x, z, me["c"], y, span] + other[x, z, y, span]
                     return carry
 
                 lax.fori_loop(0, RING * RING, one, 0)
@@ -449,12 +476,12 @@
             far, near, back = bufs[((2 - ring) * 4 + stream) * 3 + p]
             at = lambda s: place(p, stream, **free, **{axis: moved(me, axis, s)[axis]})
             if stage % 3 == 0:
-                state[p, stream, ring, "far"] = links.push(held(total, at(2), u0, n), far, moved(me, axis, way))
-                state[p, stream, ring, "back"] = links.push(held(total, at(-way), u0, n), back, moved(me, axis, -way))
+                state[p, stream, ring, "far"] = links.push(held(at(2), u0, n), far, moved(me, axis, way))
+                state[p, stream, ring, "back"] = links.push(held(at(-way), u0, n), back, moved(me, axis, -way))
             elif stage % 3 == 1:
                 state[p, stream, ring, "far"].wait_recv()
                 add(at(way), u0, n, far, lead)
-                state[p, stream, ring, "near"] = links.push(held(total, at(way), u0, n), near, moved(me, axis, way))
+                state[p, stream, ring, "near"] = links.push(held(at(way), u0, n), near, moved(me, axis, way))
             else:
                 state[p, stream, ring, "back"].wait_recv()
                 add(at(0), u0, n, back, lead)
@@ -462,23 +489,23 @@
                 add(at(0), u0, n, near, lead)
                 if ring == 1 and step != 0:
                     state[p, stream, "last"] = links.push(
-                        held(total, place(p, stream), u0, n), bufs[24 + stream * 3 + p][0], moved(me, order[0], step)
+                        held(place(p, stream), u0, n), bufs[24 + stream * 3 + p][0], moved(me, order[0], step)
                     )
     for stream in range(3):
         for p, (u0, n, order) in enumerate(ROW_PARTS):
             state[p, stream, "last"].wait_recv()
             add(me, u0, n, bufs[24 + stream * 3 + p][0], None)
-    done = from_units(total[me["x"], me["z"], me["y"]], out.shape[0])
+    done = from_units(terms[me["x"], me["z"], me["c"], me["y"]], out.shape[0])
     out_v[...] = (mid[...].astype(f32) + done.astype(f32)).astype(bf16)
-    write = pltpu.make_async_copy(out_v, out, local_sem.at[12])
+    write = pltpu.make_async_copy(out_v, out, local_sem)
     write.start()
     write.wait()
     links.finish()
 
 
-def row_sum(terms, mid):
+def row_sum(slot, made, mid):
     rows, cols = mid.shape
-    units = terms.shape[4]
+    units = rows * cols // (UNIT[0] * UNIT[1])
     n = 12 + 3 * (4 * 6 + 3)
     bufs = []
     for ring in (2, 1):
@@ -489,18 +516,19 @@
         for _, count, _ in ROW_PARTS:
             bufs += [(count,) + UNIT]
 
-    def kernel(terms, mid, out, total, other, *rest):
+    def kernel(slot, source, mid, out, terms, made, other, *rest):
         flat, rest = rest[: len(bufs)], rest[len(bufs) :]
         sets = [flat[3 * k : 3 * k + 3] for k in range(24)] + [flat[72 + k : 73 + k] for k in range(9)]
-        row_sum_kernel(terms, mid, out, total, other, sets, *rest)
+        row_sum_kernel(slot, source, mid, out, terms, made, other, sets, *rest)
 
     return pl.pallas_call(
         kernel,
         out_shape=jax.ShapeDtypeStruct((rows, cols), bf16),
-        in_specs=[ANY, WHOLE],
+        in_specs=[WHOLE, ANY, WHOLE],
         out_specs=ANY,
         scratch_shapes=[
-            pltpu.VMEM((RING, RING, RING, units) + UNIT, bf16),
+            pltpu.VMEM((RING, RING, 2, RING, units) + UNIT, bf16),
+            pltpu.VMEM(made.shape, bf16),
             pltpu.VMEM((RING, RING, RING, units) + UNIT, bf16),
         ]
         + [pltpu.VMEM(shape, bf16) for shape in bufs]
@@ -508,13 +536,14 @@
             pltpu.VMEM((rows, cols), bf16),
             pltpu.SemaphoreType.DMA((n,)),
             pltpu.SemaphoreType.DMA((n,)),
-            pltpu.SemaphoreType.DMA((13,)),
+            pltpu.SemaphoreType.DMA,
+            pltpu.SemaphoreType.DMA((RING,)),
         ],
         compiler_params=pltpu.CompilerParams(
-            collective_id=3, has_side_effects=True, vmem_limit_bytes=48 << 20
+            collective_id=3, has_side_effects=True, vmem_limit_bytes=58 << 20
         ),
         name="row_sum",
-    )(terms, mid)
+    )(slot, made, mid)
 
 
 def attend_kernel(
@@ -646,7 +675,7 @@
 PAIR = 2
 
 
-def expert_kernel(slot, gates, rows, w_gate, w_up, w_down, out, packed, scale, wgu, wd, sems):
+def expert_kernel(slot, gates, rows, w_gate, w_up, w_down, made, packed, scale, wgu, wd, sems, out_sems):
     step = pl.program_id(0)
     groups = 8
     tokens = groups * UNIT[0]
@@ -667,71 +696,61 @@
             load.start()
 
     row = lax.broadcasted_iota(jnp.int32, (pair_cap, PAIR * tokens), 0).astype(f32)
-    picks = []
     for z in range(RING):
-        span = slice(z * pair_cap, (z + 1) * pair_cap)
-        same = [
-            jnp.broadcast_to(slot[e, pl.ds(step * RING + z, 1), :], row.shape) == row for e in range(n_exp)
-        ]
+        span = pl.ds(pl.multiple_of((step * RING + z) * pair_cap, 16), pair_cap)
+        same = [jnp.broadcast_to(slot[e, pl.ds(step * RING + z, 1), :], row.shape) == row for e in range(n_exp)]
         for e in range(n_exp):
             scale[e, span, :] = jnp.sum(
                 jnp.where(same[e], gates[e, pl.ds(step * RING + z, 1), :], 0.0), axis=1, keepdims=True
             )
-        picks.append(jnp.concatenate([m.astype(f32) for m in same], axis=0).astype(bf16))
+        pick = jnp.concatenate([m.astype(f32) for m in same], axis=0).astype(bf16)
         for h in range(2):
             parts = []
             for k in range(2):
                 for j in range(tiles):
                     units = slice(j * groups, (j + 1) * groups)
                     parts.append(rows[0, z, :, 2 * h + k, units].reshape(PAIR * tokens, 128))
-            got = jnp.dot(picks[z], jnp.concatenate(parts, axis=1), preferred_element_type=f32).astype(bf16)
+            got = jnp.dot(pick, jnp.concatenate(parts, axis=1), preferred_element_type=f32).astype(bf16)
             for e in range(n_exp):
                 packed[e, span, 2 * h * quarter : 2 * (h + 1) * quarter] = got[e * pair_cap : (e + 1) * pair_cap]
 
-    @pl.when(step == 0)
+    @pl.when(step == RING - 1)
     def _():
         for load in loads:
             load.wait()
-
-    for e in range(n_exp):
-        both = jnp.dot(packed[e], wgu[e], preferred_element_type=f32)
-        gate_term, up_term = both[:, :ff], both[:, ff:]
-        act = (gate_term / (1.0 + jnp.exp(-gate_term)) * up_term).astype(bf16)
-        for h in range(2):
-            cols = slice(2 * h * quarter, 2 * (h + 1) * quarter)
-            down = jnp.dot(act, wd[e, :, cols], preferred_element_type=f32)
-            packed[e, :, cols] = (down * scale[e]).astype(bf16)
-    for z in range(RING):
-        span = slice(z * pair_cap, (z + 1) * pair_cap)
-        for h in range(2):
-            cols = slice(2 * h * quarter, 2 * (h + 1) * quarter)
-            made = jnp.concatenate([packed[e, span, cols] for e in range(n_exp)], axis=0)
-            back = lax.dot_general(picks[z], made, (((0,), (0,)), ((), ())), preferred_element_type=f32).astype(bf16)
-            for k in range(2):
-                for j in range(tiles):
-                    n = k * tiles + j
-                    out[0, z, :, 2 * h + k, j * groups : (j + 1) * groups] = back[:, n * 128 : (n + 1) * 128].reshape(
-                        PAIR, groups, *UNIT
-                    )
+        stores = []
+        for e in range(n_exp):
+            both = jnp.dot(packed[e], wgu[e], preferred_element_type=f32)
+            gate_term, up_term = both[:, :ff], both[:, ff:]
+            act = (gate_term / (1.0 + jnp.exp(-gate_term)) * up_term).astype(bf16)
+            for h in range(2):
+                cols = slice(2 * h * quarter, 2 * (h + 1) * quarter)
+                down = jnp.dot(act, wd[e, :, cols], preferred_element_type=f32)
+                packed[e, :, cols] = (down * scale[e]).astype(bf16)
+            stores.append(pltpu.make_async_copy(packed.at[e], made.at[e], out_sems.at[e]))
+            stores[e].start()
+        for store in stores:
+            store.wait()
 
 
 def experts(slot, gates, rows, w_gate, w_up, w_down):
     n_exp, width, ff = w_gate.shape
-    taken = (n_exp, RING * PAIR * CAP)
+    taken = (n_exp, RING * RING * PAIR * CAP)
     whole = pl.BlockSpec(slot.shape, lambda i: (0, 0, 0))
     some = pl.BlockSpec((1,) + rows.shape[1:], lambda i: (i,) + (0,) * (len(rows.shape) - 1))
     return pl.pallas_call(
         expert_kernel,
         grid=(RING,),
         in_specs=[whole, whole, some, ANY, ANY, ANY],
-        out_specs=some,
-        out_shape=jax.ShapeDtypeStruct(rows.shape, bf16),
+        out_specs=ANY,
+        out_shape=jax.ShapeDtypeStruct(taken + (width,), bf16),
         scratch_shapes=[
             pltpu.VMEM(taken + (width,), bf16),
             pltpu.VMEM(taken + (1,), f32),
             pltpu.VMEM((n_exp, width, 2 * ff), bf16),
             pltpu.VMEM(w_down.shape, bf16),
             pltpu.SemaphoreType.DMA((3,)),
+            pltpu.SemaphoreType.DMA((n_exp,)),
         ],
         compiler_params=pltpu.CompilerParams(vmem_limit_bytes=56 << 20),
         name="experts",
@@ -757,7 +776,7 @@
     )
     rows, mid = row_gather(terms, hidden, gain_moe.reshape(-1, 128))
     made = experts(slot, gates, rows, w_gate, w_up, w_down)
-    return (row_sum(made, mid), kv_cache)
+    return (row_sum(slot, made, mid), kv_cache)
 
 
 def solution(mesh):

time: 191 us -> 196 us (1.026)
  Pallas kernels: 186 us -> 190 us
    pallas_call x1, Pallas kernels: 54.5 us -> 64 us  [row_sum(): pl.pallas_call(kernel, out_shape=jax.ShapeDtypeStruct((rows, cols), bf16)...]
    pallas_call x1, Pallas kernels: 34 us -> 27.6 us  [experts(): pl.pallas_call(expert_kernel, grid=(RING,), in_specs=[whole, whole, some,...]
where the time goes in v4:
time: 196 us
  Pallas kernels  190 us (97%)
  local copies, waits for them, and re-layouts  4.62 us (2%)
    pallas_call x1, Pallas kernels, row_gather(): pl.pallas_call(row_gather_kernel, out_shape=(jax.ShapeDtypeStruct((RING,...  64.7 us
    pallas_call x1, Pallas kernels, row_sum(): pl.pallas_call(kernel, out_shape=jax.ShapeDtypeStruct((rows, cols), bf16)...  64 us
    pallas_call x1, Pallas kernels, experts(): pl.pallas_call(expert_kernel, grid=(RING,), in_specs=[whole, whole, some,...  27.6 us
    pallas_call x1, Pallas kernels, front(): pl.pallas_call(front_kernel, out_shape=(jax.ShapeDtypeStruct((RING, RING,...  24.3 us
    pallas_call x1, Pallas kernels, attend(): pl.pallas_call(attend_kernel, grid_spec=pltpu.PrefetchScalarGridSpec(num_...  9.09 us

profile of v4, /device:TPU:0, one launch (start us, length us, event | category | flops | bytes accessed | tf_op | source)
XLA Modules:
  0.0 195.6 jit_solution(8690075324003916084)
XLA Ops:
  0.6 0.6 pad_add_fusion.where
  1.2 1.3 dynamic_slice.3.pages
  2.5 24.3 %front.1 = (bf16[4,4,2,144,256]{4,3,2,1,0:T(8,128)(2,1)}, bf16[128,640]{1,0:T(8,128)(2,1)}, s32[128,1]{1,0:T(8,128)}) custom-call(s32[16]{0:T(128)} %lengths.1, bf16[128,2560]{1,0:T(8,128)(2,1)} %hidden.3, f32[20,128]{1,0:T(8,128)} %bitcast.9, f32[1,128]{1,0:T(1,128)} %constant.23.inverse, s32[6,128]{1,0:T(8,128)} %bitcast.10, f32[6,128]{1,0:T(8,128)} %bitcast.11, ...), custom_call_target="tpu_custom_call" | custom-call | tf_op jit(solution)/shard_map/front/pallas_call | solution.py:283
  26.8 0.0 copy-start
  26.9 0.0 copy-start.3
  26.9 9.1 %attend.1 = (bf16[4,128,640]{2,1,0:T(8,128)(2,1)}, bf16[64,16,256]{2,1,0:T(8,128)(2,1)}, f32[2,16,256]{2,1,0:T(8,128)}, f32[2,16,256]{2,1,0:T(8,128)}) custom-call(s32[2]{0:T(128)} %pad_add_fusion.where, s32[64]{0:T(128)} %dynamic_slice.3.pages, bf16[128,640]{1,0:T(8,128)(2,1)} %get-tuple-element.11.queries, s32[128,1]{1,0:T(8,128)} %get-tuple-element.12.first, ...), custom_call_target="tpu_custom_call" | custom-call | tf_op jit(solution)/shard_map/attend/pallas_call | solution.py:648
  36.0 0.0 copy-done
  36.0 0.0 copy-done.3
  36.0 0.0 copy-start.1
  36.0 1.1 copy-done.1
  37.1 64.7 %row_gather.1 = (bf16[4,4,2,4,40,16,128]{6,5,4,3,2,1,0:T(8,128)(2,1)}, bf16[128,640]{1,0:T(8,128)(2,1)S(1)}) custom-call(bf16[4,128,640]{2,1,0:T(8,128)(2,1)S(1)} %copy-done.1, bf16[128,2560]{1,0:T(8,128)(2,1)S(1)} %copy-done, f32[20,128]{1,0:T(8,128)S(1)} %bitcast.7), custom_call_target="tpu_custom_call" | custom-call | tf_op jit(solution)/shard_map/row_gather/pallas_call | solution.py:351
  101.7 0.0 copy-start.2
  101.7 0.7 copy-done.2
  102.4 27.6 %experts.1.source = bf16[2,768,2560]{2,1,0:T(8,128)(2,1)} custom-call(f32[2,16,256]{2,1,0:T(8,128)} %get-tuple-element.14.slot, f32[2,16,256]{2,1,0:T(8,128)} %get-tuple-element.15.gates, bf16[4,4,2,4,40,16,128]{6,5,4,3,2,1,0:T(8,128)(2,1)} %get-tuple-element.17.rows, bf16[2,2560,384]{2,1,0:T(8,128)(2,1)} %w_gate.1, bf16[2,2560,384]{2,1,0:T(8,128)(2,1)} %w_up.1, ...), custom_call_target="tpu_custom_call" | custom-call | tf_op jit(solution)/shard_map/experts/pallas_call | solution.py:741
  130.0 64.0 %row_sum.1 = bf16[128,640]{1,0:T(8,128)(2,1)} custom-call(f32[2,16,256]{2,1,0:T(8,128)} %get-tuple-element.14.slot, bf16[2,768,2560]{2,1,0:T(8,128)(2,1)} %experts.1.source, bf16[128,640]{1,0:T(8,128)(2,1)} %copy-done.2), custom_call_target="tpu_custom_call" | custom-call | tf_op jit(solution)/shard_map/row_sum/pallas_call | solution.py:524
  194.0 1.6 copy.18
Async XLA Ops:
  26.8 9.1 %copy-start = (bf16[128,2560]{1,0:T(8,128)(2,1)S(1)}, bf16[128,2560]{1,0:T(8,128)(2,1)}, u32[]{:S(2)}) copy-start(bf16[128,2560]{1,0:T(8,128)(2,1)} %hidden.3) | copy-start | bytes 1966084
  26.9 9.1 %copy-start.3 = (f32[2560]{0:T(1024)S(1)}, f32[2560]{0:T(1024)}, u32[]{:S(2)}) copy-start(f32[2560]{0:T(1024)} %param.21) | copy-start | bytes 30724
  36.0 1.1 copy-start.1
  101.7 0.7 copy-start.2

commit v5 on v4

--- a/solution.py
+++ b/solution.py
@@ -411,12 +411,19 @@
                     )
 
     def one_chip(chip, carry):
-        spread(chip // RING, lax.rem(chip, RING))
+        spread(chip // RING, chip % RING)
         return carry
 
+    exchanged = []
     for x in range(RING):
         takes[x].wait()
-        lax.fori_loop(x * RING, (x + 1) * RING, one_chip, 0)
+        if x < RING - 1:
+            lax.fori_loop(x * RING, (x + 1) * RING, one_chip, 0)
+            exchanged.append(links.push(terms.at[x, :, sibling["c"]], other.at[x], sibling))
+            continue
+        for z in range(RING):
+            one_chip(x * RING + z, 0)
+            exchanged.append(links.push(terms.at[x, z, sibling["c"]], other.at[x, z], sibling))
 
     def held(where, u0, n):
         return terms.at[where["x"], where["z"], me["c"], where["y"], pl.ds(u0, n)]
@@ -428,16 +435,6 @@
         where.update(free)
         return where
 
-    first = {}
-    for stream in range(4):
-        for p, (u0, n, order) in enumerate(ROW_PARTS):
-            where = place(p, stream, **{order[1]: slice(None), order[2]: slice(None)})
-            first[p, stream] = links.push(
-                terms.at[where["x"], where["z"], sibling["c"], where["y"], pl.ds(u0, n)],
-                other.at[where["x"], where["z"], where["y"], pl.ds(u0, n)],
-                sibling,
-            )
-
     def add(where, u0, n, buf, lead):
         span = pl.ds(u0, n)
         if lead is None:
@@ -458,7 +455,9 @@
         step, way = SUM_STREAMS[stream]
         for p, (u0, n, order) in enumerate(ROW_PARTS):
             if stage == 0:
-                first[p, stream].wait_recv()
+                if stream == 0 and p == 0:
+                    for push in exchanged:
+                        push.wait_recv()
                 where = place(p, stream)
                 span = pl.ds(u0, n)
 
@@ -506,7 +505,7 @@
 def row_sum(slot, made, mid):
     rows, cols = mid.shape
     units = rows * cols // (UNIT[0] * UNIT[1])
-    n = 12 + 3 * (4 * 6 + 3)
+    n = 2 * RING - 1 + 3 * (4 * 6 + 3)
     bufs = []
     for ring in (2, 1):
         for stream in range(4):

time: 196 us -> 202 us (1.031)
  Pallas kernels: 190 us -> 196 us
    pallas_call x1, Pallas kernels: 64 us -> 70.3 us  [row_sum(): pl.pallas_call(kernel, out_shape=jax.ShapeDtypeStruct((rows, cols), bf16)...]
where the time goes in v5:
time: 202 us
  Pallas kernels  196 us (97%)
  local copies, waits for them, and re-layouts  4.62 us (2%)
    pallas_call x1, Pallas kernels, row_sum(): pl.pallas_call(kernel, out_shape=jax.ShapeDtypeStruct((rows, cols), bf16)...  70.3 us
    pallas_call x1, Pallas kernels, row_gather(): pl.pallas_call(row_gather_kernel, out_shape=(jax.ShapeDtypeStruct((RING,...  64.7 us
    pallas_call x1, Pallas kernels, experts(): pl.pallas_call(expert_kernel, grid=(RING,), in_specs=[whole, whole, some,...  27.6 us
    pallas_call x1, Pallas kernels, front(): pl.pallas_call(front_kernel, out_shape=(jax.ShapeDtypeStruct((RING, RING,...  24.3 us
    pallas_call x1, Pallas kernels, attend(): pl.pallas_call(attend_kernel, grid_spec=pltpu.PrefetchScalarGridSpec(num_...  9.09 us

profile of v5, /device:TPU:0, one launch (start us, length us, event | category | flops | bytes accessed | tf_op | source)
XLA Modules:
  0.0 202.0 jit_solution(16206897789491015393)
XLA Ops:
  0.6 0.6 pad_add_fusion.where
  1.2 1.3 dynamic_slice.3.pages
  2.5 24.3 %front.1 = (bf16[4,4,2,144,256]{4,3,2,1,0:T(8,128)(2,1)}, bf16[128,640]{1,0:T(8,128)(2,1)}, s32[128,1]{1,0:T(8,128)}) custom-call(s32[16]{0:T(128)} %lengths.1, bf16[128,2560]{1,0:T(8,128)(2,1)} %hidden.3, f32[20,128]{1,0:T(8,128)} %bitcast.9, f32[1,128]{1,0:T(1,128)} %constant.23.inverse, s32[6,128]{1,0:T(8,128)} %bitcast.10, f32[6,128]{1,0:T(8,128)} %bitcast.11, ...), custom_call_target="tpu_custom_call" | custom-call | tf_op jit(solution)/shard_map/front/pallas_call | solution.py:283
  26.8 0.0 copy-start
  26.9 0.0 copy-start.3
  26.9 9.1 %attend.1 = (bf16[4,128,640]{2,1,0:T(8,128)(2,1)}, bf16[64,16,256]{2,1,0:T(8,128)(2,1)}, f32[2,16,256]{2,1,0:T(8,128)}, f32[2,16,256]{2,1,0:T(8,128)}) custom-call(s32[2]{0:T(128)} %pad_add_fusion.where, s32[64]{0:T(128)} %dynamic_slice.3.pages, bf16[128,640]{1,0:T(8,128)(2,1)} %get-tuple-element.11.queries, s32[128,1]{1,0:T(8,128)} %get-tuple-element.12.first, ...), custom_call_target="tpu_custom_call" | custom-call | tf_op jit(solution)/shard_map/attend/pallas_call | solution.py:647
  36.0 0.0 copy-done
  36.0 0.0 copy-done.3
  36.0 0.0 copy-start.1
  36.0 1.1 copy-done.1
  37.1 64.7 %row_gather.1 = (bf16[4,4,2,4,40,16,128]{6,5,4,3,2,1,0:T(8,128)(2,1)}, bf16[128,640]{1,0:T(8,128)(2,1)S(1)}) custom-call(bf16[4,128,640]{2,1,0:T(8,128)(2,1)S(1)} %copy-done.1, bf16[128,2560]{1,0:T(8,128)(2,1)S(1)} %copy-done, f32[20,128]{1,0:T(8,128)S(1)} %bitcast.7), custom_call_target="tpu_custom_call" | custom-call | tf_op jit(solution)/shard_map/row_gather/pallas_call | solution.py:351
  101.7 0.0 copy-start.2
  101.7 0.7 copy-done.2
  102.4 27.6 %experts.1.source = bf16[2,768,2560]{2,1,0:T(8,128)(2,1)} custom-call(f32[2,16,256]{2,1,0:T(8,128)} %get-tuple-element.14.slot, f32[2,16,256]{2,1,0:T(8,128)} %get-tuple-element.15.gates, bf16[4,4,2,4,40,16,128]{6,5,4,3,2,1,0:T(8,128)(2,1)} %get-tuple-element.17.rows, bf16[2,2560,384]{2,1,0:T(8,128)(2,1)} %w_gate.1, bf16[2,2560,384]{2,1,0:T(8,128)(2,1)} %w_up.1, ...), custom_call_target="tpu_custom_call" | custom-call | tf_op jit(solution)/shard_map/experts/pallas_call | solution.py:740
  130.0 70.3 %row_sum.1 = bf16[128,640]{1,0:T(8,128)(2,1)} custom-call(f32[2,16,256]{2,1,0:T(8,128)} %get-tuple-element.14.slot, bf16[2,768,2560]{2,1,0:T(8,128)(2,1)} %experts.1.source, bf16[128,640]{1,0:T(8,128)(2,1)} %copy-done.2), custom_call_target="tpu_custom_call" | custom-call | tf_op jit(solution)/shard_map/row_sum/pallas_call | solution.py:523
  200.4 1.6 copy.18
Async XLA Ops:
  26.8 9.1 %copy-start = (bf16[128,2560]{1,0:T(8,128)(2,1)S(1)}, bf16[128,2560]{1,0:T(8,128)(2,1)}, u32[]{:S(2)}) copy-start(bf16[128,2560]{1,0:T(8,128)(2,1)} %hidden.3) | copy-start | bytes 1966084
  26.9 9.1 %copy-start.3 = (f32[2560]{0:T(1024)S(1)}, f32[2560]{0:T(1024)}, u32[]{:S(2)}) copy-start(f32[2560]{0:T(1024)} %param.21) | copy-start | bytes 30724
  36.0 1.1 copy-start.1
  101.7 0.7 copy-start.2
